TPU v7x, 128 devices: a whole 4x4x4 slice. The times are simulated.
128 devices in a mesh: row: 8 (over x, y_hi), col: 16 (over y_lo, z, core).
Axes of the slice: x: 4, y: 4 (y_hi: 2, y_lo: 2; y = y_hi * 2 + y_lo), z: 4, core: 2. Of those that a mesh axis runs over, the one named last changes fastest.
Arguments:
- tokens: bfloat16 [768, 8192], P('row', 'col'), may hold values from -6 to 6
- weight_in: bfloat16 [8192, 32768], P('col', 'row'), may hold values from -0.125 to 0.125
- mask_in: int32 [64, 256], P('col', 'row'), may hold values 0 or 1
- weight_out: bfloat16 [32768, 8192], P('row', 'col'), may hold values from -0.0625 to 0.0625
- mask_out: int32 [256, 64], P('row', 'col'), may hold values 0 or 1
- cotangent: bfloat16 [768, 8192], P('row', 'col'), may hold values from -6 to 6
Outputs:
- result: bfloat16 [768, 8192], P('row', 'col')
- tokens_grad: bfloat16 [768, 8192], P('row', 'col')
- weight_in_grad: bfloat16 [8192, 32768], P('col', 'row')
- weight_out_grad: bfloat16 [32768, 8192], P('row', 'col')
All inputs are finite; a program needn't handle non-finite values. No bound on the sum of `mask_in` or of `mask_out` on one device may be relied on, other than what follows from the above.
Results may differ from a plain program's by a relative error of at most 0.005.
Values may be sent and summed in bfloat16 or wider, within the bound.
A program may use at most 128 MiB of HBM per device.

v0:
```python
import jax
import jax.numpy as jnp
from jax import lax
from jax.sharding import PartitionSpec as P

BLOCK = 128


root_two_pi = 0.7978845608
cubic_coef = 0.044715


def in_one_piece(arrays, axis, dim, along):
    widths = [a.shape[along] for a in arrays]
    both = jnp.concatenate(arrays, axis=along)
    whole = lax.all_gather(both, axis, axis=dim, tiled=True)
    return tuple(jnp.split(whole, [sum(widths[:k]) for k in range(1, len(widths))], axis=along))


def in_blocks(shard, dim, count):
    before, after = (shard.shape[:dim], shard.shape[dim + 1 :])
    return jnp.moveaxis(shard.reshape(*before, count, -1, *after), dim, 0)


def sent_and_summed(shard, axis, dim):
    parts = in_blocks(shard, dim, lax.axis_size(axis))
    arrived = lax.all_to_all(parts, axis, split_axis=0, concat_axis=0, tiled=True)
    return arrived.sum(axis=0)


def expand(mask):
    blocks_a, blocks_b = mask.shape
    spread = mask.astype(jnp.bfloat16)
    return jnp.broadcast_to(spread[:, None, :, None], (blocks_a, BLOCK, blocks_b, BLOCK)).reshape(
        blocks_a * BLOCK, blocks_b * BLOCK
    )


def gelu_value(values):
    tangent = jnp.tanh(root_two_pi * (values + cubic_coef * values * values * values))
    return 0.5 * values * (1.0 + tangent)


def gelu_slope(values):
    tangent = jnp.tanh(root_two_pi * (values + cubic_coef * values * values * values))
    return 0.5 * (1.0 + tangent) + 0.5 * values * (1.0 - tangent * tangent) * root_two_pi * (
        1.0 + 3.0 * cubic_coef * values * values
    )


def contract(left, right, left_dim, right_dim):
    return lax.dot_general(
        left, right, (((left_dim,), (right_dim,)), ((), ())), preferred_element_type=jnp.float32
    )


def body(tokens, weight_in, mask_in, weight_out, mask_out, cotangent):
    block_in = expand(mask_in)
    block_out = expand(mask_out)
    masked_in = weight_in * block_in
    masked_out = weight_out * block_out
    tokens_all, cotangent_all = in_one_piece((tokens, cotangent), "row", 0, 1)
    selected = tokens_all
    preact = lax.psum_scatter(
        jnp.dot(selected, masked_in, preferred_element_type=jnp.float32),
        "col",
        scatter_dimension=0,
        tiled=True,
    )
    hidden_all = lax.all_gather(gelu_value(preact).astype(jnp.bfloat16), "col", axis=0, tiled=True)
    selected = hidden_all
    result = sent_and_summed(
        jnp.dot(selected, masked_out, preferred_element_type=jnp.float32), "row", 0
    ).astype(jnp.bfloat16)
    selected = cotangent_all
    hidden_grad = lax.psum_scatter(
        contract(selected, masked_out, 1, 1), "col", scatter_dimension=0, tiled=True
    )
    preact_grad = lax.all_gather(
        (hidden_grad * gelu_slope(preact)).astype(jnp.bfloat16), "col", axis=0, tiled=True
    )
    selected = preact_grad
    tokens_grad = sent_and_summed(contract(selected, masked_in, 1, 1), "row", 0).astype(
        jnp.bfloat16
    )
    weight_in_grad = (contract(tokens_all, preact_grad, 0, 0) * block_in).astype(jnp.bfloat16)
    weight_out_grad = (contract(hidden_all, cotangent_all, 0, 0) * block_out).astype(jnp.bfloat16)
    return (result, tokens_grad, weight_in_grad, weight_out_grad)


def solution(mesh):
    return jax.shard_map(
        body,
        mesh=mesh,
        in_specs=(
            P("row", "col"),
            P("col", "row"),
            P("col", "row"),
            P("row", "col"),
            P("row", "col"),
            P("row", "col"),
        ),
        out_specs=(P("row", "col"), P("row", "col"), P("col", "row"), P("row", "col")),
        check_vma=False,
    )
```

profile of v0, /device:TPU:0, one launch (start us, length us, event | category | flops | bytes accessed | tf_op | source)
XLA Modules:
  0.0 394.2 jit_solution(3372894636051000812)
XLA Ops:
  7.2 0.0 all-gather.4.cloned.1.call-start
  7.2 1.6 pad_maximum_fusion
  8.9 0.0 reduce-scatter.5.cloned.1.call-start
  8.9 0.7 convert_element_type.32
  9.6 0.1 copy.10
  9.7 54.6 %all-gather.4.cloned.1.call-done = bf16[768,1024]{1,0:T(8,128)(2,1)} async-done(((bf16[96,1024]{1,0:T(8,128)(2,1)}), bf16[768,1024]{1,0:T(8,128)(2,1)}) %all-gather.4.cloned.1.call-update) | async-done | bytes 1572880 | tf_op jit(solution)/shard_map/all_gather | solution.py:16
  64.3 1.1 broadcast_in_dim.5
  65.5 2.0 copy-done.1
  67.5 7.6 %fusion.2 = f32[768,4096]{1,0:T(8,128)} fusion(bf16[4096,512]{1,0:T(8,128)(2,1)S(1)} %copy-done.3, bf16[512,8,4,128]{3,2,1,0:T(4,128)(2,1)S(1)} %bitcast.23, bf16[768,1024]{1,0:T(8,128)(2,1)} %all-gather.4.cloned.1.call-done), kind=kOutput, calls=%fused_computation.8 | convolution fusion | flops 3223322624 | bytes 21757952 | tf_op jit(solution)/shard_map/dot_general | solution.py:52
  75.2 0.0 reduce-scatter.3.cloned.1.call-start
  75.2 0.6 copy-done.7
  75.8 0.6 broadcast_in_dim.4
  76.4 2.1 copy-done
  78.6 1.0 copy-done.4
  79.6 8.8 %fusion.1 = f32[768,4096]{1,0:T(8,128)} fusion(bf16[512,4096]{1,0:T(8,128)(2,1)S(1)} %copy-done.4, bf16[64,8,32,128]{3,2,1,0:T(8,128)(2,1)S(1)} %bitcast.20, bf16[768,1024]{1,0:T(8,128)(2,1)S(1)} %copy-done.5), kind=kOutput, calls=%fused_computation.7 | convolution fusion | flops 3223322624 | bytes 21757952 | tf_op jit(solution)/shard_map/dot_general | solution.py:65
  88.4 0.0 all-gather.6.cloned.1.call-start
  88.5 68.2 %reduce-scatter.5.cloned.1.call-done = f32[48,4096]{1,0:T(8,128)} async-done(((f32[768,4096]{1,0:T(8,128)}), f32[48,4096]{1,0:T(8,128)}) %reduce-scatter.5.cloned.1.call-update) | async-done | bytes 786448 | tf_op jit(solution)/shard_map/reduce_scatter | solution.py:76
  156.7 83.8 %reduce-scatter.3.cloned.1.call-done = f32[48,4096]{1,0:T(8,128)} async-done(((f32[768,4096]{1,0:T(8,128)}), f32[48,4096]{1,0:T(8,128)}) %reduce-scatter.3.cloned.1.call-update) | async-done | bytes 786448 | tf_op jit(solution)/shard_map/reduce_scatter | solution.py:64
  240.5 2.8 fusion.10
  243.4 0.0 all-gather.8.cloned.1.call-start
  243.4 0.5 all-gather.8.cloned.1.call-update
  244.0 40.9 %all-gather.6.cloned.1.call-done = bf16[768,4096]{1,0:T(8,128)(2,1)} async-done(((bf16[48,4096]{1,0:T(8,128)(2,1)}), bf16[768,4096]{1,0:T(8,128)(2,1)}) %all-gather.6.cloned.1.call-update) | async-done | bytes 6291472 | tf_op jit(solution)/shard_map/all_gather | solution.py:70
  284.8 9.8 %fusion.3 = f32[768,512]{1,0:T(8,128)} fusion(bf16[768,4096]{1,0:T(8,128)(2,1)} %all-gather.6.cloned.1.call-done, bf16[4096,512]{1,0:T(8,128)(2,1)} %param.9, bf16[512,8,4,128]{3,2,1,0:T(4,128)(2,1)} %bitcast.24), kind=kOutput, calls=%fused_computation.9 | convolution fusion | flops 3223322624 | bytes 16252928 | tf_op jit(solution)/shard_map/dot_general | solution.py:73
  294.7 6.5 %all-to-all-start = ((f32[8,96,512]{2,1,0:T(8,128)}), f32[8,96,512]{2,1,0:T(8,128)S(1)}, u32[]{:S(2)}, u32[]{:S(2)}) async-start(f32[8,96,512]{2,1,0:T(8,128)} %bitcast), calls=%async_computation.1 | async-start | bytes 3145728 | tf_op jit(solution)/shard_map/all_to_all | solution.py:27
  301.1 45.0 %all-gather.8.cloned.1.call-done = bf16[768,4096]{1,0:T(8,128)(2,1)} async-done(((bf16[48,4096]{1,0:T(8,128)(2,1)}), bf16[768,4096]{1,0:T(8,128)(2,1)}) %all-gather.8.cloned.1.call-update) | async-done | bytes 6291472 | tf_op jit(solution)/shard_map/all_gather | solution.py:79
  346.1 10.0 %fusion = f32[768,512]{1,0:T(8,128)} fusion(bf16[768,4096]{1,0:T(8,128)(2,1)} %all-gather.8.cloned.1.call-done, bf16[512,4096]{1,0:T(8,128)(2,1)} %param.7, bf16[64,8,32,128]{3,2,1,0:T(8,128)(2,1)} %bitcast.21), kind=kOutput, calls=%fused_computation.6 | convolution fusion | flops 3223322624 | bytes 16252928 | tf_op jit(solution)/shard_map/dot_general | solution.py:52
  356.1 6.4 %all-to-all-start.1 = ((f32[8,96,512]{2,1,0:T(8,128)}), f32[8,96,512]{2,1,0:T(8,128)S(1)}, u32[]{:S(2)}, u32[]{:S(2)}) async-start(f32[8,96,512]{2,1,0:T(8,128)} %bitcast.26), calls=%async_computation.3 | async-start | bytes 3145728 | tf_op jit(solution)/shard_map/all_to_all | solution.py:27
  362.6 10.8 %multiply_convert_fusion.1 = bf16[512,4096]{1,0:T(8,128)(2,1)} fusion(bf16[768,4096]{1,0:T(8,128)(2,1)} %all-gather.8.cloned.1.call-done, bf16[64,8,32,128]{3,2,1,0:T(8,128)(2,1)} %bitcast.22, bf16[768,1024]{1,0:T(8,128)(2,1)} %all-gather.4.cloned.1.call-done), kind=kOutput, calls=%fused_computation.1 | convolution fusion | flops 3227516928 | bytes 15466496 | tf_op jit(solution)/shard_map/dot_general | solution.py:52
  373.4 8.8 %multiply_convert_fusion = bf16[4096,512]{1,0:T(8,128)(2,1)} fusion(bf16[768,4096]{1,0:T(8,128)(2,1)} %all-gather.6.cloned.1.call-done, bf16[512,8,4,128]{3,2,1,0:T(4,128)(2,1)S(1)} %bitcast.25, bf16[768,1024]{1,0:T(8,128)(2,1)S(1)} %copy-done.6), kind=kOutput, calls=%fused_computation | convolution fusion | flops 3227516928 | bytes 15466496 | tf_op jit(solution)/shard_map/dot_general | solution.py:52
  382.2 0.8 reduce_sum.18
  383.0 3.9 all-to-all-done.1
  386.9 0.8 reduce_sum.19
  (18 shorter events, 0.1 us)
Async XLA Ops:
  7.2 57.2 %all-gather.4.cloned.1.call-start = ((), (), s32[]{:S(2)}) async-start(), calls=%async_computation.4 | async-start | bytes 1769472 | tf_op jit(solution)/shard_map/all_gather | solution.py:16
  8.9 147.8 %reduce-scatter.5.cloned.1.call-start = ((), (), s32[]{:S(2)}) async-start(), calls=%async_computation.7 | async-start | bytes 13369344 | tf_op jit(solution)/shard_map/reduce_scatter | solution.py:76
  64.3 3.2 copy-start.3
  65.5 2.0 copy-start.1
  75.1 0.7 copy-start.7
  75.1 3.4 copy-start.5
  75.2 165.4 %reduce-scatter.3.cloned.1.call-start = ((), (), s32[]{:S(2)}) async-start(), calls=%async_computation.5 | async-start | bytes 13369344 | tf_op jit(solution)/shard_map/reduce_scatter | solution.py:64
  75.8 3.8 copy-start.4
  76.4 2.1 copy-start
  88.4 196.4 %all-gather.6.cloned.1.call-start = ((), (), s32[]{:S(2)}) async-start(), calls=%async_computation.6 | async-start | bytes 6684672 | tf_op jit(solution)/shard_map/all_gather | solution.py:70
  243.4 102.7 %all-gather.8.cloned.1.call-start = ((), (), s32[]{:S(2)}) async-start(), calls=%async_computation.8 | async-start | bytes 6684672 | tf_op jit(solution)/shard_map/all_gather | solution.py:79
  294.7 61.5 %all-to-all-start = ((f32[8,96,512]{2,1,0:T(8,128)}), f32[8,96,512]{2,1,0:T(8,128)S(1)}, u32[]{:S(2)}, u32[]{:S(2)}) async-start(f32[8,96,512]{2,1,0:T(8,128)} %bitcast), calls=%async_computation.1 | async-start | bytes 3145728 | tf_op jit(solution)/shard_map/all_to_all | solution.py:27
  356.1 30.7 %all-to-all-start.1 = ((f32[8,96,512]{2,1,0:T(8,128)}), f32[8,96,512]{2,1,0:T(8,128)S(1)}, u32[]{:S(2)}, u32[]{:S(2)}) async-start(f32[8,96,512]{2,1,0:T(8,128)} %bitcast.26), calls=%async_computation.3 | async-start | bytes 3145728 | tf_op jit(solution)/shard_map/all_to_all | solution.py:27
  362.5 10.9 %copy-start.2 = (bf16[32,128,4,128]{3,2,1,0:T(4,128)(2,1)S(1)}, bf16[32,128,4,128]{3,2,1,0:T(4,128)(2,1)}, u32[]{:S(2)}) copy-start(bf16[32,128,4,128]{3,2,1,0:T(4,128)(2,1)} %copy-done.1) | copy-start | bytes 12582916
  362.5 10.9 %copy-start.6 = (bf16[768,1024]{1,0:T(8,128)(2,1)S(1)}, bf16[768,1024]{1,0:T(8,128)(2,1)}, u32[]{:S(2)}) copy-start(bf16[768,1024]{1,0:T(8,128)(2,1)} %all-gather.4.cloned.1.call-done) | copy-start | bytes 4718596
Sparse Core Ops, SparseCore 0:
  10.9 53.4 all-gather.3
  75.3 81.3 reduce-scatter.4
  159.1 81.3 reduce-scatter.2
  243.5 41.3 all-gather.5
  286.4 59.6 all-gather.7
where the time goes:
time: 395 us; the launch traced here: 394 us
  waiting for transfers between devices  297 us (75%)
  matrix products  55.9 us (14%)
  between operations  13.8 us (3%)
  starting transfers between devices  13.1 us (3%)
  local copies, waits for them, and re-layouts  7.63 us (2%)
  other arithmetic  6.69 us (2%)
    reduce_scatter x1, waiting for transfers between devices, body(): lax.psum_scatter(jnp.dot(selected, masked_in, preferred_element_type=jnp....  83.8 us
    reduce_scatter x1, waiting for transfers between devices, body(): lax.psum_scatter(contract(selected, masked_out, 1, 1), 'col', scatter_dim...  68.2 us
    all_gather x1, waiting for transfers between devices, in_one_piece(): whole = lax.all_gather(both, axis, axis=dim, tiled=True)  54.6 us
    all_gather x1, waiting for transfers between devices, body(): lax.all_gather((hidden_grad * gelu_slope(preact)).astype(jnp.bfloat16), '...  45 us
    all_gather x1, waiting for transfers between devices, body(): lax.all_gather(gelu_value(preact).astype(jnp.bfloat16), 'col', axis=0, ti...  40.9 us
    dot_general x4, matrix products, contract(): lax.dot_general(left, right, (((left_dim,), (right_dim,)), ((), ())), pre...  37.3 us
    all_to_all x2, starting transfers between devices, sent_and_summed(): lax.all_to_all(parts, axis, split_axis=0, concat_axis=0, tiled=True)  12.9 us
    dot_general x1, matrix products, body(): jnp.dot(selected, masked_out, preferred_element_type=jnp.float32)  9.82 us
  transfers between devices with their start and end apart: 7, of which 6 were waited for; matrix products, arithmetic and copies ran while one was open for 13% of the time, Pallas kernels for 0%

commit v1 on v0

v1 whole, which is shorter than its diff:
```python
import jax
import jax.numpy as jnp
from jax import lax
from jax.experimental import pallas as pl
from jax.experimental.pallas import tpu as pltpu
from jax.sharding import PartitionSpec as P

BLOCK = 128
CHUNKS = 8
WIDE = 256
BF = jnp.bfloat16
F32 = jnp.float32

root_two_pi = 0.7978845608
cubic_coef = 0.044715

ORDERS = ((0, 2, 1), (1, 2, 0), (2, 0, 1), (0, 1, 2), (1, 0, 2), (2, 1, 0), (0, 2, 1), (1, 2, 0))


def dot(left, right, left_dim, right_dim):
    return lax.dot_general(
        left, right, (((left_dim,), (right_dim,)), ((), ())), preferred_element_type=F32
    )


def gelu_both(values):
    tangent = jnp.tanh(root_two_pi * (values + cubic_coef * values * values * values))
    value = 0.5 * values * (1.0 + tangent)
    slope = 0.5 * (1.0 + tangent) + 0.5 * values * (1.0 - tangent * tangent) * root_two_pi * (
        1.0 + 3.0 * cubic_coef * values * values
    )
    return value, slope


N_COPIES = 160


def kernel(
    tok, cot, win, wout, mi, mo,
    res_o, tg_o, dwi_o, dwo_o,
    TA, CA, WI, WO, SI, SO,
    S1a, R1a, ACa, S2a, R2a, S3a, R3a,
    S1b, R1b, ACb, S2b, R2b, S3b, R3b,
    H, G, R, RX, T1, U1, T2, U2, T3, U3, OUT,
    send_sem, recv_sem, local_sem,
):
    row = lax.axis_index("row")
    col = lax.axis_index("col")
    x, yh = lax.div(row, 2), lax.rem(row, 2)
    yl = lax.div(col, 8)
    z = lax.div(lax.rem(col, 8), 2)
    core = lax.rem(col, 2)
    xb, xa = lax.div(x, 2), lax.rem(lax.div(x + 1, 2), 2)
    zb, za = lax.div(z, 2), lax.rem(lax.div(z + 1, 2), 2)
    here = {"row": row, "col": col}
    at_core = {"row": row, "col": col + 1 - 2 * core}
    at_y = {"row": row, "col": col + 8 - 16 * yl}
    at_za = {"row": row, "col": col + 2 * (1 - 2 * lax.rem(z, 2))}
    at_zb = {"row": row, "col": col + 2 * (3 - 2 * z)}
    at_xa = {"row": row + 2 * (1 - 2 * lax.rem(x, 2)), "col": col}
    at_xb = {"row": row + 2 * (3 - 2 * x), "col": col}
    at_yh = {"row": row + 1 - 2 * yh, "col": col}
    del here
    bits = (yl, za, zb)
    partner = (at_y, at_za, at_zb)

    count = [0]
    sent = []

    def push(src, dst, where):
        k = count[0]
        count[0] += 1
        copy = pltpu.make_async_remote_copy(
            src_ref=src, dst_ref=dst, send_sem=send_sem.at[k], recv_sem=recv_sem.at[k],
            device_id=where, device_id_type=pl.DeviceIdType.MESH,
        )
        copy.start()
        sent.append(copy)
        return copy

    lcount = [0]

    def local(src, dst):
        k = lcount[0]
        lcount[0] += 1
        copy = pltpu.make_async_copy(src, dst, local_sem.at[k])
        copy.start()
        return copy

    tok_in = local(tok, TA.at[core, xb, xa, yh])
    cot_in = local(cot, CA.at[core, xb, xa, yh])
    si_in = [local(win.at[:, pl.ds(h * 2048, 2048)], SI.at[h]) for h in range(2)]
    so_in = [local(wout.at[pl.ds(h * 2048, 2048)], SO.at[h]) for h in range(2)]

    barrier = pltpu.get_barrier_semaphore()
    for where in (at_core, at_y, at_za, at_zb, at_xa, at_xb, at_yh):
        pl.semaphore_signal(barrier, inc=1, device_id=where, device_id_type=pl.DeviceIdType.MESH)
    pl.semaphore_wait(barrier, 7)

    def gather_first(A):
        c = {}
        c["y"] = push(A.at[core, xb, xa, yh], A.at[core, xb, xa, yh], at_yh)
        c["a0"] = push(A.at[core, xb, xa, yh, 0], A.at[core, xb, xa, yh, 0], at_xb)
        c["b0"] = push(A.at[core, xb, xa, yh, 1], A.at[core, xb, xa, yh, 1], at_xa)
        return c

    def gather_second(A, c, v, tag):
        c["a" + tag].wait_recv()
        c["A" + tag] = push(A.at[core, :, xa, v, 0], A.at[core, :, xa, v, 0], at_xa)
        c["b" + tag].wait_recv()
        c["B" + tag] = push(A.at[core, xb, :, v, 1], A.at[core, xb, :, v, 1], at_xb)

    def gather_third(A, c, v):
        c["y"].wait_recv()
        c["a1"] = push(A.at[core, xb, xa, v, 0], A.at[core, xb, xa, v, 0], at_xb)
        c["b1"] = push(A.at[core, xb, xa, v, 1], A.at[core, xb, xa, v, 1], at_xa)

    def gather_cross(A, c, v, tag):
        c["A" + tag].wait_recv()
        c["B" + tag].wait_recv()
        c["c" + tag] = push(A.at[core, :, :, v], A.at[core, :, :, v], at_core)

    tok_in.wait()
    tc = gather_first(TA)
    cot_in.wait()
    cc = gather_first(CA)

    other = 1 - core

    def mask_in_half(h, dst):
        def step(i, carry):
            r = pl.multiple_of(i * BLOCK, BLOCK)
            m = mi[i, :, pl.ds(pl.multiple_of(h * 2048, 2048), 2048)]
            w = SI[h, pl.ds(r, BLOCK), :].reshape(8, 16, 2048)
            dst[pl.ds(r, BLOCK), :] = (w * m[None]).reshape(BLOCK, 2048)
            return carry
        lax.fori_loop(0, 4, step, 0)

    def mask_out_half(h, dst):
        def step(i, carry):
            r = pl.multiple_of(i * BLOCK, BLOCK)
            m = mo[h * 16 + i]
            w = SO[h, pl.ds(r, BLOCK), :].reshape(8, 16, 512)
            dst[pl.ds(r, BLOCK), :] = (w * m[None]).reshape(BLOCK, 512)
            return carry
        lax.fori_loop(0, 16, step, 0)

    for c in si_in:
        c.wait()
    mask_in_half(other, SI.at[other])
    wi_c = push(SI.at[other], WI.at[core], at_core)
    gather_second(TA, tc, yh, "0")
    gather_third(TA, tc, 1 - yh)
    mask_in_half(core, WI.at[core])
    for c in so_in:
        c.wait()
    mask_out_half(other, SO.at[other])
    wo_c = push(SO.at[other], WO.at[core], at_core)
    gather_second(TA, tc, 1 - yh, "1")
    gather_cross(TA, tc, yh, "0")
    gather_second(CA, cc, yh, "0")
    gather_third(CA, cc, 1 - yh)
    mask_out_half(core, WO.at[core])
    gather_cross(TA, tc, 1 - yh, "1")
    gather_second(CA, cc, 1 - yh, "1")
    wi_c.wait_recv()
    tc["c0"].wait_recv()
    tc["c1"].wait_recv()

    def part_in(j, half):
        out = None
        for k in range(2):
            t = dot(TA[k, half].reshape(384, 512), WI[k, :, WIDE * j : WIDE * (j + 1)], 1, 0)
            out = t if out is None else out + t
        return out.reshape(4, 96, WIDE)

    def part_out(j, half):
        out = None
        for k in range(2):
            t = dot(CA[k, half].reshape(384, 512), WO[k, WIDE * j : WIDE * (j + 1), :], 1, 1)
            out = t if out is None else out + t
        return out.reshape(4, 96, WIDE)

    streams = ((part_in, S1a, R1a, ACa, S2a, R2a, S3a, R3a), (part_out, S1b, R1b, ACb, S2b, R2b, S3b, R3b))
    first = [[None] * CHUNKS for _ in range(2)]
    second = [[None] * CHUNKS for _ in range(2)]
    third = [[None] * CHUNKS for _ in range(2)]

    def halve_first(s, j):
        part, S1, R1, AC, S2, R2, S3, R3 = streams[s]
        d = ORDERS[j][0]
        S1[j] = part(j, 1 - bits[d]).astype(BF)
        first[s][j] = push(S1.at[j], R1.at[j], partner[d])

    def halve_kept(s, j):
        part, S1, R1, AC, S2, R2, S3, R3 = streams[s]
        AC[j] = part(j, bits[ORDERS[j][0]])

    def halve_second(s, j):
        part, S1, R1, AC, S2, R2, S3, R3 = streams[s]
        d = ORDERS[j][1]
        away, keep = 2 * (1 - bits[d]), 2 * bits[d]
        first[s][j].wait_recv()
        S2[j] = (AC[j, pl.ds(away, 2)] + R1[j, pl.ds(away, 2)].astype(F32)).astype(BF)
        second[s][j] = push(S2.at[j], R2.at[j], partner[d])
        AC[j, pl.ds(keep, 2)] = AC[j, pl.ds(keep, 2)] + R1[j, pl.ds(keep, 2)].astype(F32)

    def halve_third(s, j):
        part, S1, R1, AC, S2, R2, S3, R3 = streams[s]
        base, d = 2 * bits[ORDERS[j][1]], ORDERS[j][2]
        away, keep = 1 - bits[d], bits[d]
        second[s][j].wait_recv()
        S3[j] = (AC[j, base + away] + R2[j, away].astype(F32)).astype(BF)
        third[s][j] = push(S3.at[j], R3.at[j], partner[d])
        AC[j, base + keep] = AC[j, base + keep] + R2[j, keep].astype(F32)

    def whole(s, j):
        part, S1, R1, AC, S2, R2, S3, R3 = streams[s]
        third[s][j].wait_recv()
        q = 2 * bits[ORDERS[j][1]] + bits[ORDERS[j][2]]
        return AC[j, q] + R3[j].astype(F32), q

    d1 = [[None] * CHUNKS for _ in range(2)]
    d2 = [[None] * CHUNKS for _ in range(2)]
    d3 = [[None] * CHUNKS for _ in range(2)]

    def double_first(s, j, A):
        m = [bits[d] for d in ORDERS[j]]
        at = A.at[j, 4 * m[0] + 2 * m[1] + m[2]]
        d1[s][j] = push(at, at, partner[ORDERS[j][2]])

    def double_second(s, j, A):
        m = [bits[d] for d in ORDERS[j]]
        d1[s][j].wait_recv()
        at = A.at[j, pl.ds(4 * m[0] + 2 * m[1], 2)]
        d2[s][j] = push(at, at, partner[ORDERS[j][1]])

    def double_third(s, j, A):
        m = [bits[d] for d in ORDERS[j]]
        d2[s][j].wait_recv()
        at = A.at[j, pl.ds(4 * m[0], 4)]
        d3[s][j] = push(at, at, partner[ORDERS[j][0]])

    def make_hidden(j):
        m = [bits[d] for d in ORDERS[j]]
        v, q = whole(0, j)
        value, slope = gelu_both(v)
        H[j, 4 * m[0] + 2 * m[1] + m[2]] = value.astype(BF)
        ACa[j, q] = slope
        double_first(0, j, H)

    def make_grad(j):
        m = [bits[d] for d in ORDERS[j]]
        v, q = whole(1, j)
        G[j, 4 * m[0] + 2 * m[1] + m[2]] = (v * ACa[j, q]).astype(BF)
        double_first(1, j, G)

    each = range(CHUNKS)
    for j in each:
        halve_first(0, j)
    gather_cross(CA, cc, yh, "0")
    for j in each:
        halve_kept(0, j)
    gather_cross(CA, cc, 1 - yh, "1")
    wo_c.wait_recv()
    cc["c0"].wait_recv()
    cc["c1"].wait_recv()
    for j in each:
        halve_first(1, j)
    for j in each:
        halve_second(0, j)
    for j in each:
        halve_kept(1, j)
    for j in each:
        halve_third(0, j)
    for j in each:
        halve_second(1, j)
    for j in each:
        make_hidden(j)
    for j in each:
        halve_third(1, j)
    for j in each:
        double_second(0, j, H)
    for j in each:
        make_grad(j)
    for j in each:
        double_third(0, j, H)
    for j in each:
        double_second(1, j, G)

    def out_part(A, group, weight_of, right_dim):
        def step(t, carry):
            k, h = lax.div(t, 2), lax.rem(t, 2)
            left = jnp.concatenate(
                [A[4 * group + i, pl.ds(4 * h, 4)].reshape(384, WIDE) for i in range(4)], axis=1
            )
            got = dot(left, weight_of(k), 1, right_dim).reshape(2, 2, 2, 48, 512)
            if group == 0:
                R[k, h] = got
            else:
                R[k, h] = R[k, h] + got
            return carry
        lax.fori_loop(0, 4, step, 0)

    def row_cross(n):
        return push(R.at[other], RX.at[n], at_core)

    def full(n, idx):
        return R[(core,) + idx] + RX[(n,) + idx]

    def row_first(cross, n):
        cross.wait_recv()
        every = slice(None)
        T1[n, 0] = full(n, (1 - xb, every, every, 0)).astype(BF)
        a = push(T1.at[n, 0], U1.at[n, 0], at_xb)
        T1[n, 1] = full(n, (every, 1 - xa, every, 1)).astype(BF)
        b = push(T1.at[n, 1], U1.at[n, 1], at_xa)
        return a, b

    def row_second(copies, n):
        every = slice(None)
        copies[0].wait_recv()
        T2[n, 0] = (full(n, (xb, 1 - xa, every, 0)) + U1[n, 0, 1 - xa].astype(F32)).astype(BF)
        a = push(T2.at[n, 0], U2.at[n, 0], at_xa)
        copies[1].wait_recv()
        T2[n, 1] = (full(n, (1 - xb, xa, every, 1)) + U1[n, 1, 1 - xb].astype(F32)).astype(BF)
        b = push(T2.at[n, 1], U2.at[n, 1], at_xb)
        return a, b

    def row_sum(n, v, hf):
        near = (xa, xb)[hf]
        return full(n, (xb, xa, v, hf)) + U1[n, hf, near, v].astype(F32) + U2[n, hf, v].astype(F32)

    def row_third(copies, n):
        copies[0].wait_recv()
        T3[n, 0] = row_sum(n, 1 - yh, 0).astype(BF)
        copies[1].wait_recv()
        T3[n, 1] = row_sum(n, 1 - yh, 1).astype(BF)
        return push(T3.at[n], U3.at[n], at_yh)

    def row_last(copy, n, out):
        copy.wait_recv()
        for hf in range(2):
            OUT[n, hf] = (row_sum(n, yh, hf) + U3[n, hf].astype(F32)).astype(BF)
        return local(OUT.at[n], out)

    def out_grad(lo, hi):
        def step(j, carry):
            left = H[j].reshape(768, WIDE)
            for k in range(2):
                got = dot(left, CA[k].reshape(768, 512), 0, 0)
                SO[k, pl.ds(pl.multiple_of(j * WIDE, WIDE), WIDE), :] = got.astype(BF)
            return carry
        lax.fori_loop(lo, hi, step, 0)

    def in_grad():
        def step(t, carry):
            k, i = lax.div(t, 2), lax.rem(t, 2)
            d = pl.multiple_of(i * WIDE, WIDE)
            left = TA[k, :, :, :, :, :, pl.ds(d, WIDE)].reshape(768, WIDE)
            for j in range(CHUNKS):
                got = dot(left, G[j].reshape(768, WIDE), 0, 0)
                SI[k, pl.ds(d, WIDE), WIDE * j : WIDE * (j + 1)] = got.astype(BF)
            return carry
        lax.fori_loop(0, 4, step, 0)

    def wout_of(group):
        return lambda k: WO[k, 1024 * group : 1024 * (group + 1), :]

    def win_of(group):
        return lambda k: WI[k, :, 1024 * group : 1024 * (group + 1)]

    for j in range(4):
        d3[0][j].wait_recv()
    out_part(H, 0, wout_of(0), 0)
    for j in range(4, 8):
        d3[0][j].wait_recv()
    out_part(H, 1, wout_of(1), 0)
    cross0 = row_cross(0)
    for j in each:
        double_third(1, j, G)
    wo_c.wait_send()
    out_grad(0, 2)
    pair = row_first(cross0, 0)
    out_grad(2, 5)
    pair = row_second(pair, 0)
    out_grad(5, 8)
    cols = pl.ds(pl.multiple_of(core * 2048, 2048), 2048)
    dwo_far = push(SO.at[other], dwo_o.at[cols], at_core)
    dwo_own = local(SO.at[core], dwo_o.at[cols])
    last = row_third(pair, 0)
    out0 = row_last(last, 0, res_o)

    cross0.wait_send()
    for j in range(4):
        d3[1][j].wait_recv()
    out_part(G, 0, win_of(0), 1)
    for j in range(4, 8):
        d3[1][j].wait_recv()
    out_part(G, 1, win_of(1), 1)
    cross = row_cross(1)
    wi_c.wait_send()
    pair = row_first(cross, 1)
    in_grad()
    dwi_far = push(SI.at[other], dwi_o.at[:, cols], at_core)
    dwi_own = local(SI.at[core], dwi_o.at[:, cols])
    pair = row_second(pair, 1)
    last = row_third(pair, 1)
    out1 = row_last(last, 1, tg_o)
    dwo_far.wait_recv()
    dwi_far.wait_recv()
    for c in (out0, out1, dwo_own, dwi_own):
        c.wait()
    for c in sent:
        if c is not wo_c and c is not wi_c and c is not cross0:
            c.wait_send()


def body(tokens, weight_in, mask_in, weight_out, mask_out, cotangent):
    mi = jnp.broadcast_to(jnp.repeat(mask_in.astype(BF), BLOCK, axis=1)[:, None], (4, 16, 4096))
    mo = jnp.broadcast_to(jnp.repeat(mask_out.astype(BF), BLOCK, axis=1)[:, None], (32, 16, 512))
    anywhere = pl.BlockSpec(memory_space=pl.ANY)
    vmem = pl.BlockSpec(memory_space=pltpu.VMEM)

    def halving():
        return [
            pltpu.VMEM((CHUNKS, 4, 96, WIDE), BF),
            pltpu.VMEM((CHUNKS, 4, 96, WIDE), BF),
            pltpu.VMEM((CHUNKS, 4, 96, WIDE), F32),
            pltpu.VMEM((CHUNKS, 2, 96, WIDE), BF),
            pltpu.VMEM((CHUNKS, 2, 96, WIDE), BF),
            pltpu.VMEM((CHUNKS, 96, WIDE), BF),
            pltpu.VMEM((CHUNKS, 96, WIDE), BF),
        ]

    result, tokens_grad, dwi, dwo = pl.pallas_call(
        kernel,
        out_shape=(
            jax.ShapeDtypeStruct((2, 48, 512), BF),
            jax.ShapeDtypeStruct((2, 48, 512), BF),
            jax.ShapeDtypeStruct((512, 4096), BF),
            jax.ShapeDtypeStruct((4096, 512), BF),
        ),
        in_specs=[anywhere] * 4 + [vmem] * 2,
        out_specs=(anywhere,) * 4,
        scratch_shapes=[
            pltpu.VMEM((2, 2, 2, 2, 2, 48, 512), BF),
            pltpu.VMEM((2, 2, 2, 2, 2, 48, 512), BF),
            pltpu.VMEM((2, 512, 2048), BF),
            pltpu.VMEM((2, 2048, 512), BF),
            pltpu.VMEM((2, 512, 2048), BF),
            pltpu.VMEM((2, 2048, 512), BF),
        ]
        + halving()
        + halving()
        + [
            pltpu.VMEM((CHUNKS, 8, 96, WIDE), BF),
            pltpu.VMEM((CHUNKS, 8, 96, WIDE), BF),
            pltpu.VMEM((2, 2, 2, 2, 2, 48, 512), F32),
            pltpu.VMEM((2, 2, 2, 2, 2, 48, 512), F32),
            pltpu.VMEM((2, 2, 2, 2, 48, 512), BF),
            pltpu.VMEM((2, 2, 2, 2, 48, 512), BF),
            pltpu.VMEM((2, 2, 2, 48, 512), BF),
            pltpu.VMEM((2, 2, 2, 48, 512), BF),
            pltpu.VMEM((2, 2, 48, 512), BF),
            pltpu.VMEM((2, 2, 48, 512), BF),
            pltpu.VMEM((2, 2, 48, 512), BF),
            pltpu.SemaphoreType.DMA((N_COPIES,)),
            pltpu.SemaphoreType.DMA((N_COPIES,)),
            pltpu.SemaphoreType.DMA((16,)),
        ],
        compiler_params=pltpu.CompilerParams(
            collective_id=0, has_side_effects=True, vmem_limit_bytes=67043328
        ),
    )(tokens.reshape(2, 48, 512), cotangent.reshape(2, 48, 512), weight_in, weight_out, mi, mo)
    dwi = (dwi.reshape(4, 8, 16, 4096) * mi[:, None]).reshape(512, 4096)
    dwo = (dwo.reshape(32, 8, 16, 512) * mo[:, None]).reshape(4096, 512)
    return result.reshape(96, 512), tokens_grad.reshape(96, 512), dwi, dwo


def solution(mesh):
    return jax.shard_map(
        body,
        mesh=mesh,
        in_specs=(
            P("row", "col"),
            P("col", "row"),
            P("col", "row"),
            P("row", "col"),
            P("row", "col"),
            P("row", "col"),
        ),
        out_specs=(P("row", "col"), P("row", "col"), P("col", "row"), P("row", "col")),
        check_vma=False,
    )
```

time: 395 us -> 154 us (0.39)
  waiting for transfers between devices: 297 us -> 0 us
  Pallas kernels: 0 us -> 139 us
  matrix products: 55.9 us -> 0 us
  starting transfers between devices: 13.1 us -> 0 us
  between operations: 13.8 us -> 0.72 us
    reduce_scatter x2 -> x0, waiting for transfers between devices: 152 us -> none  [the longest x1 83.8 us: body(): lax.psum_scatter(jnp.dot(selected, masked_in, preferred_element_type=jnp....]
    all_gather x3 -> x0, waiting for transfers between devices: 140 us -> none  [the longest x1 54.6 us: in_one_piece(): whole = lax.all_gather(both, axis, axis=dim, tiled=True)]
    pallas_call x0 -> x1, Pallas kernels: none -> 139 us  [body(): pl.pallas_call(kernel, out_shape=(jax.ShapeDtypeStruct((2, 48, 512), BF),...]
    dot_general x6 -> x0, matrix products: 55.9 us -> none  [the longest x4 37.3 us: contract(): lax.dot_general(left, right, (((left_dim,), (right_dim,)), ((), ())), pre...]
    all_to_all x2 -> x0, starting transfers between devices: 12.9 us -> none  [sent_and_summed(): lax.all_to_all(parts, axis, split_axis=0, concat_axis=0, tiled=True)]
    mul x0 -> x2, other arithmetic: none -> 6.94 us  [the longest x1 4.64 us: body(): dwi = (dwi.reshape(4, 8, 16, 4096) * mi[:, None]).reshape(512, 4096)]
  transfers between devices with their start and end apart: 7 -> 0, of which waited for: 6 -> 0; matrix products, arithmetic and copies ran while one was open for 13% -> 0% of each run, Pallas kernels for 0% -> 0%
where the time goes in v1:
time: 154 us; the launch traced here: 152 us
  Pallas kernels  139 us (90%)
  other arithmetic  8.31 us (5%)
  local copies, waits for them, and re-layouts  3.89 us (3%)
    pallas_call x1, Pallas kernels, body(): pl.pallas_call(kernel, out_shape=(jax.ShapeDtypeStruct((2, 48, 512), BF),...  139 us
    mul x1, other arithmetic, body(): dwi = (dwi.reshape(4, 8, 16, 4096) * mi[:, None]).reshape(512, 4096)  4.64 us

profile of v1, /device:TPU:0, one launch (start us, length us, event | category | flops | bytes accessed | tf_op | source)
XLA Modules:
  0.0 151.9 jit_solution(6073101695531120863)
XLA Ops:
  0.6 0.7 convert_element_type.6
  1.3 0.7 convert_element_type.7
  2.0 0.1 copy.10
  2.1 0.1 broadcast_in_dim.23
  2.2 0.0 copy-start.1
  2.2 0.1 broadcast_bitcast_fusion
  2.4 0.0 copy-start.3
  2.4 0.6 copy-done.3
  3.0 0.8 broadcast_in_dim.22.mi
  3.8 0.0 copy-done.1
  3.8 0.8 broadcast_in_dim.25.mo
  4.6 139.0 %shard_map.93 = (bf16[2,48,512]{2,1,0:T(8,128)(2,1)}, bf16[2,48,512]{2,1,0:T(8,128)(2,1)}, bf16[512,4096]{1,0:T(8,128)(2,1)}, bf16[4096,512]{1,0:T(8,128)(2,1)}) custom-call(bf16[2,48,512]{2,1,0:T(8,128)(2,1)} %bitcast.22, bf16[2,48,512]{2,1,0:T(8,128)(2,1)} %bitcast.23, bf16[512,4096]{1,0:T(8,128)(2,1)} %win.1, bf16[4096,512]{1,0:T(8,128)(2,1)} %wout.1, ...), custom_call_target="tpu_custom_call" | custom-call | tf_op jit(solution)/shard_map/pallas_call | solution.py:436
  143.6 0.0 copy-start
  143.6 0.0 copy-start.2
  143.6 4.6 %bitcast_multiply_fusion.1 = bf16[512,4096]{1,0:T(8,128)(2,1)} fusion(bf16[512,4096]{1,0:T(8,128)(2,1)} %get-tuple-element.10, bf16[4,4096]{1,0:T(4,128)(2,1)} %bitcast.20), kind=kLoop, calls=%fused_computation.1 | loop fusion | flops 2097152 | bytes 8421376 | tf_op jit(solution)/shard_map/mul | solution.py:476
  148.3 0.0 copy-done
  148.3 0.0 copy-done.2
  148.3 0.0 copy-start.5
  148.3 0.0 copy-start.4
  148.3 2.3 %bitcast_multiply_fusion = bf16[4096,512]{1,0:T(8,128)(2,1)} fusion(bf16[4096,512]{1,0:T(8,128)(2,1)S(1)} %copy-done, bf16[32,512]{1,0:T(8,128)(2,1)S(1)} %bitcast.18), kind=kLoop, calls=%fused_computation | loop fusion | flops 2097152 | bytes 8421376 | tf_op jit(solution)/shard_map/mul | solution.py:477
  150.6 0.0 copy-done.5
  150.6 0.6 copy.19
  151.2 0.0 copy-done.4
  151.2 0.6 copy.20
  (2 shorter events, 0.0 us)
Async XLA Ops:
  2.2 1.6 %copy-start.1 = (bf16[4,8,4,128]{3,1,2,0:T(8,128)(2,1)}, bf16[4,8,4,128]{3,1,2,0:T(8,128)(2,1)S(1)}, u32[]{:S(2)}) copy-start(bf16[4,8,4,128]{3,1,2,0:T(8,128)(2,1)S(1)} %copy.15) | copy-start | bytes 98308
  2.4 0.6 copy-start.3
  143.6 4.7 %copy-start = (bf16[4096,512]{1,0:T(8,128)(2,1)S(1)}, bf16[4096,512]{1,0:T(8,128)(2,1)}, u32[]{:S(2)}) copy-start(bf16[4096,512]{1,0:T(8,128)(2,1)} %get-tuple-element.11) | copy-start | bytes 12582916
  143.6 4.7 %copy-start.2 = (bf16[4,8,4,128]{3,1,2,0:T(8,128)(2,1)S(1)}, bf16[4,8,4,128]{3,1,2,0:T(8,128)(2,1)}, u32[]{:S(2)}) copy-start(bf16[4,8,4,128]{3,1,2,0:T(8,128)(2,1)} %copy-done.1) | copy-start | bytes 98308
  148.3 2.3 %copy-start.5 = (bf16[2,48,512]{2,1,0:T(8,128)(2,1)S(1)}, bf16[2,48,512]{2,1,0:T(8,128)(2,1)}, u32[]{:S(2)}) copy-start(bf16[2,48,512]{2,1,0:T(8,128)(2,1)} %get-tuple-element.8) | copy-start | bytes 294916
  148.3 3.0 %copy-start.4 = (bf16[2,48,512]{2,1,0:T(8,128)(2,1)S(1)}, bf16[2,48,512]{2,1,0:T(8,128)(2,1)}, u32[]{:S(2)}) copy-start(bf16[2,48,512]{2,1,0:T(8,128)(2,1)} %get-tuple-element.9) | copy-start | bytes 294916

commit v2 on v1

v2 whole, which is shorter than its diff:
```python
import jax
import jax.numpy as jnp
from jax import lax
from jax.experimental import pallas as pl
from jax.experimental.pallas import tpu as pltpu
from jax.sharding import PartitionSpec as P

BLOCK = 128
CHUNKS = 8
WIDE = 256
BF = jnp.bfloat16
F32 = jnp.float32

root_two_pi = 0.7978845608
cubic_coef = 0.044715

ORDERS = ((0, 2, 1), (1, 2, 0), (2, 0, 1), (0, 1, 2), (1, 0, 2), (2, 1, 0), (0, 2, 1), (1, 2, 0))


def dot(left, right, left_dim, right_dim):
    return lax.dot_general(
        left, right, (((left_dim,), (right_dim,)), ((), ())), preferred_element_type=F32
    )


def gelu_both(values):
    tangent = jnp.tanh(root_two_pi * (values + cubic_coef * values * values * values))
    value = 0.5 * values * (1.0 + tangent)
    slope = 0.5 * (1.0 + tangent) + 0.5 * values * (1.0 - tangent * tangent) * root_two_pi * (
        1.0 + 3.0 * cubic_coef * values * values
    )
    return value, slope
OUT_KIND = pltpu.VMEM
VMEM_BYTES = 49 * 1024 * 1024


N_COPIES = 192


def kernel(
    tok, cot, win, wout, mask_in, mask_out_t,
    res_o, tg_o, DI, DO,
    TA, CA, WI, WO, FI, FO, MIS, MI, MOS, MO,
    S1a, R1a, ACa, S2a, R2a, S3a, R3a,
    S1b, R1b, ACb, S2b, R2b, S3b, R3b,
    H, G, R, RX, T1, U1, T2, U2, T3, U3, KEEP,
    send_sem, recv_sem, local_sem,
):
    row = lax.axis_index("row")
    col = lax.axis_index("col")
    x, yh = lax.div(row, 2), lax.rem(row, 2)
    yl = lax.div(col, 8)
    z = lax.div(lax.rem(col, 8), 2)
    core = lax.rem(col, 2)
    other = 1 - core
    xb, xa = lax.div(x, 2), lax.rem(lax.div(x + 1, 2), 2)
    zb, za = lax.div(z, 2), lax.rem(lax.div(z + 1, 2), 2)
    at_core = {"row": row, "col": col + 1 - 2 * core}
    at_y = {"row": row, "col": col + 8 - 16 * yl}
    at_za = {"row": row, "col": col + 2 * (1 - 2 * lax.rem(z, 2))}
    at_zb = {"row": row, "col": col + 2 * (3 - 2 * z)}
    at_xa = {"row": row + 2 * (1 - 2 * lax.rem(x, 2)), "col": col}
    at_xb = {"row": row + 2 * (3 - 2 * x), "col": col}
    at_yh = {"row": row + 1 - 2 * yh, "col": col}
    bits = (yl, za, zb)
    partner = (at_y, at_za, at_zb)

    count = [0]
    sent = []

    def push(src, dst, where):
        k = count[0]
        count[0] += 1
        copy = pltpu.make_async_remote_copy(
            src_ref=src, dst_ref=dst, send_sem=send_sem.at[k], recv_sem=recv_sem.at[k],
            device_id=where, device_id_type=pl.DeviceIdType.MESH,
        )
        copy.start()
        sent.append(copy)
        return copy

    lcount = [0]

    def local(src, dst):
        k = lcount[0]
        lcount[0] += 1
        copy = pltpu.make_async_copy(src, dst, local_sem.at[k])
        copy.start()
        return copy

    def cols(h):
        return pl.ds(pl.multiple_of(h * 2048, 2048), 2048)

    barrier = pltpu.get_barrier_semaphore()
    for where in (at_core, at_y, at_za, at_zb, at_xa, at_xb, at_yh):
        pl.semaphore_signal(barrier, inc=1, device_id=where, device_id_type=pl.DeviceIdType.MESH)

    tok_in = local(tok, TA.at[core, xb, xa, yh])
    cot_in = local(cot, CA.at[core, xb, xa, yh])
    si_far = local(win.at[:, cols(other)], DI.at[:, cols(other)])
    si_own = local(win.at[:, cols(core)], DI.at[:, cols(core)])
    so_far = local(wout.at[cols(other)], DO.at[cols(other)])
    so_own = local(wout.at[cols(core)], DO.at[cols(core)])

    def spread(scalar):
        return jnp.full((16, BLOCK), scalar.astype(F32), F32).astype(BF)

    def expand_in(h, dst):
        def step(j, carry):
            for i in range(4):
                dst[i, :, pl.ds(pl.multiple_of(j * BLOCK, BLOCK), BLOCK)] = spread(
                    mask_in[i, h * 16 + j]
                )
            return carry
        lax.fori_loop(0, 16, step, 0)

    def expand_out(h, dst):
        def step(i, carry):
            for j in range(4):
                dst[i, :, BLOCK * j : BLOCK * (j + 1)] = spread(mask_out_t[j, h * 16 + i])
            return carry
        lax.fori_loop(0, 16, step, 0)

    expand_in(other, MIS)
    expand_in(core, MI.at[core])
    expand_out(other, MOS)
    expand_out(core, MO.at[core])
    pl.semaphore_wait(barrier, 7)

    def gather_y(A):
        return {"y": push(A.at[core, xb, xa, yh], A.at[core, xb, xa, yh], at_yh)}

    def gather_first(A, c):
        c["a0"] = push(A.at[core, xb, xa, yh, 0], A.at[core, xb, xa, yh, 0], at_xb)
        c["b0"] = push(A.at[core, xb, xa, yh, 1], A.at[core, xb, xa, yh, 1], at_xa)

    def gather_second(A, c, v, tag):
        c["a" + tag].wait_recv()
        c["A" + tag] = push(A.at[core, :, xa, v, 0], A.at[core, :, xa, v, 0], at_xa)
        c["b" + tag].wait_recv()
        c["B" + tag] = push(A.at[core, xb, :, v, 1], A.at[core, xb, :, v, 1], at_xb)

    def gather_third(A, c, v):
        c["y"].wait_recv()
        c["a1"] = push(A.at[core, xb, xa, v, 0], A.at[core, xb, xa, v, 0], at_xb)
        c["b1"] = push(A.at[core, xb, xa, v, 1], A.at[core, xb, xa, v, 1], at_xa)

    def gather_cross(A, c, v, tag):
        c["A" + tag].wait_recv()
        c["B" + tag].wait_recv()
        c["c" + tag] = push(A.at[core, :, :, v], A.at[core, :, :, v], at_core)

    def mask_in_half(h, m, dst):
        def step(i, carry):
            r = pl.multiple_of(i * BLOCK, BLOCK)
            w = DI[pl.ds(r, BLOCK), cols(h)].reshape(8, 16, 2048)
            dst[pl.ds(r, BLOCK), :] = (w * m[i][None]).reshape(BLOCK, 2048)
            return carry
        lax.fori_loop(0, 4, step, 0)

    def mask_out_half(h, m, dst):
        def step(i, carry):
            r = pl.multiple_of(i * BLOCK, BLOCK)
            w = DO[pl.ds(pl.multiple_of(h * 2048 + r, BLOCK), BLOCK), :].reshape(8, 16, 512)
            dst[pl.ds(r, BLOCK), :] = (w * m[i][None]).reshape(BLOCK, 512)
            return carry
        lax.fori_loop(0, 16, step, 0)

    tok_in.wait()
    tc = gather_y(TA)
    gather_first(TA, tc)
    cot_in.wait()
    cc = gather_y(CA)
    si_far.wait()
    mask_in_half(other, MIS, FI)
    wi_c = push(FI, WI.at[core], at_core)
    gather_second(TA, tc, yh, "0")
    gather_first(CA, cc)
    si_own.wait()
    mask_in_half(core, MI.at[core], WI.at[core])
    so_far.wait()
    mask_out_half(other, MOS, FO)
    gather_cross(TA, tc, yh, "0")
    wo_c = push(FO, WO.at[core], at_core)
    gather_third(TA, tc, 1 - yh)
    wi_c.wait_recv()
    tc["c0"].wait_recv()

    def part_rows(j, half, v):
        out = None
        for k in range(2):
            t = dot(TA[k, half, :, v].reshape(192, 512), WI[k, :, WIDE * j : WIDE * (j + 1)], 1, 0)
            out = t if out is None else out + t
        return out.reshape(2, 96, WIDE)

    def part_in(j, half):
        out = None
        for k in range(2):
            t = dot(TA[k, half].reshape(384, 512), WI[k, :, WIDE * j : WIDE * (j + 1)], 1, 0)
            out = t if out is None else out + t
        return out.reshape(2, 2, 96, WIDE)

    def part_out(j, half):
        out = None
        for k in range(2):
            t = dot(CA[k, half].reshape(384, 512), WO[k, WIDE * j : WIDE * (j + 1), :], 1, 1)
            out = t if out is None else out + t
        return out.reshape(2, 2, 96, WIDE)

    streams = ((part_in, S1a, R1a, ACa, S2a, R2a, S3a, R3a), (part_out, S1b, R1b, ACb, S2b, R2b, S3b, R3b))
    first = [[None] * CHUNKS for _ in range(2)]
    second = [[None] * CHUNKS for _ in range(2)]
    third = [[None] * CHUNKS for _ in range(2)]

    def halve_rows(j, v):
        d = ORDERS[j][0]
        S1a[j, :, v] = part_rows(j, 1 - bits[d], v).astype(BF)
        c = push(S1a.at[j, :, v], R1a.at[j, :, v], partner[d])
        first[0][j] = (first[0][j] or ()) + (c,)

    def halve_first(s, j):
        part, S1, R1, AC, S2, R2, S3, R3 = streams[s]
        d = ORDERS[j][0]
        S1[j] = part(j, 1 - bits[d]).astype(BF)
        first[s][j] = (push(S1.at[j], R1.at[j], partner[d]),)

    def halve_kept(s, j):
        part, S1, R1, AC, S2, R2, S3, R3 = streams[s]
        AC[j] = part(j, bits[ORDERS[j][0]])

    def halve_second(s, j):
        part, S1, R1, AC, S2, R2, S3, R3 = streams[s]
        d = ORDERS[j][1]
        away, keep = 1 - bits[d], bits[d]
        for c in first[s][j]:
            c.wait_recv()
        S2[j] = (AC[j, away] + R1[j, away].astype(F32)).astype(BF)
        second[s][j] = push(S2.at[j], R2.at[j], partner[d])
        AC[j, keep] = AC[j, keep] + R1[j, keep].astype(F32)

    def halve_third(s, j):
        part, S1, R1, AC, S2, R2, S3, R3 = streams[s]
        base, d = bits[ORDERS[j][1]], ORDERS[j][2]
        away, keep = 1 - bits[d], bits[d]
        second[s][j].wait_recv()
        S3[j] = (AC[j, base, away] + R2[j, away].astype(F32)).astype(BF)
        third[s][j] = push(S3.at[j], R3.at[j], partner[d])
        AC[j, base, keep] = AC[j, base, keep] + R2[j, keep].astype(F32)

    def whole(s, j):
        part, S1, R1, AC, S2, R2, S3, R3 = streams[s]
        third[s][j].wait_recv()
        base, last = bits[ORDERS[j][1]], bits[ORDERS[j][2]]
        return AC[j, base, last] + R3[j].astype(F32), base, last

    d1 = [[None] * CHUNKS for _ in range(2)]
    d2 = [[None] * CHUNKS for _ in range(2)]
    d3 = [[None] * CHUNKS for _ in range(2)]

    def double_first(s, j, A):
        m = [bits[d] for d in ORDERS[j]]
        at = A.at[j, 4 * m[0] + 2 * m[1] + m[2]]
        d1[s][j] = push(at, at, partner[ORDERS[j][2]])

    def double_second(s, j, A):
        m = [bits[d] for d in ORDERS[j]]
        d1[s][j].wait_recv()
        at = A.at[j, pl.ds(4 * m[0] + 2 * m[1], 2)]
        d2[s][j] = push(at, at, partner[ORDERS[j][1]])

    def double_third(s, j, A):
        m = [bits[d] for d in ORDERS[j]]
        d2[s][j].wait_recv()
        at = A.at[j, pl.ds(4 * m[0], 4)]
        d3[s][j] = push(at, at, partner[ORDERS[j][0]])

    def make_hidden(j):
        m = [bits[d] for d in ORDERS[j]]
        v, base, last = whole(0, j)
        value, slope = gelu_both(v)
        H[j, 4 * m[0] + 2 * m[1] + m[2]] = value.astype(BF)
        ACa[j, base, last] = slope
        double_first(0, j, H)

    def make_grad(j):
        m = [bits[d] for d in ORDERS[j]]
        v, base, last = whole(1, j)
        G[j, 4 * m[0] + 2 * m[1] + m[2]] = (v * ACa[j, base, last]).astype(BF)
        double_first(1, j, G)

    each = range(CHUNKS)
    for j in range(4):
        halve_rows(j, yh)
    gather_second(TA, tc, 1 - yh, "1")
    for j in range(4, 8):
        halve_rows(j, yh)
    gather_second(CA, cc, yh, "0")
    gather_third(CA, cc, 1 - yh)
    gather_cross(TA, tc, 1 - yh, "1")
    so_own.wait()
    mask_out_half(core, MO.at[core], WO.at[core])
    tc["c1"].wait_recv()
    for j in range(4):
        halve_rows(j, 1 - yh)
    gather_second(CA, cc, 1 - yh, "1")
    gather_cross(CA, cc, yh, "0")
    for j in range(4, 8):
        halve_rows(j, 1 - yh)
    for j in range(4):
        halve_kept(0, j)
    gather_cross(CA, cc, 1 - yh, "1")
    mi_c = push(MIS, MI.at[core], at_core)
    mo_c = push(MOS, MO.at[core], at_core)
    for j in range(4, 8):
        halve_kept(0, j)
    wo_c.wait_recv()
    cc["c0"].wait_recv()
    cc["c1"].wait_recv()
    for j in each:
        halve_first(1, j)
    for j in each:
        halve_second(0, j)
    for j in each:
        halve_kept(1, j)
    for j in each:
        halve_third(0, j)
    for j in each:
        halve_second(1, j)
    for j in each:
        make_hidden(j)
    for j in each:
        halve_third(1, j)
    for j in each:
        double_second(0, j, H)
    for j in each:
        make_grad(j)
    for j in each:
        double_third(0, j, H)
    for j in each:
        double_second(1, j, G)

    every = slice(None)

    def lanes(u):
        return slice(256 * u, 256 * (u + 1))

    def out_part(A, lo, hi, u, k, weight, right_dim):
        def step(h, carry):
            left = jnp.concatenate(
                [A[i, pl.ds(4 * h, 4)].reshape(384, WIDE) for i in range(lo, hi)], axis=1
            )
            got = dot(left, weight(lo, hi, u, k), 1, right_dim).reshape(2, 2, 2, 48, 256)
            if lo == 0:
                R[k, u, h] = got
            else:
                R[k, u, h] = R[k, u, h] + got
            return carry
        lax.fori_loop(0, 2, step, 0)

    def wout_of(lo, hi, u, k):
        return WO[k, WIDE * lo : WIDE * hi, lanes(u)]

    def win_of(lo, hi, u, k):
        return WI[k, lanes(u), WIDE * lo : WIDE * hi]

    def row_cross(n, u):
        return push(R.at[other, u], RX.at[n, u], at_core)

    def full(n, u, idx):
        return R[(core, u) + idx] + RX[(n, u) + idx]

    def row_first(cross, n, u):
        cross.wait_recv()
        T1[n, u, 0] = full(n, u, (1 - xb, every, every, 0)).astype(BF)
        a = push(T1.at[n, u, 0], U1.at[n, u, 0], at_xb)
        T1[n, u, 1] = full(n, u, (every, 1 - xa, every, 1)).astype(BF)
        b = push(T1.at[n, u, 1], U1.at[n, u, 1], at_xa)
        return a, b

    def row_second(copies, n, u):
        copies[0].wait_recv()
        T2[n, u, 0] = (full(n, u, (xb, 1 - xa, every, 0)) + U1[n, u, 0, 1 - xa].astype(F32)).astype(BF)
        a = push(T2.at[n, u, 0], U2.at[n, u, 0], at_xa)
        copies[1].wait_recv()
        T2[n, u, 1] = (full(n, u, (1 - xb, xa, every, 1)) + U1[n, u, 1, 1 - xb].astype(F32)).astype(BF)
        b = push(T2.at[n, u, 1], U2.at[n, u, 1], at_xb)
        return a, b

    def row_third(copies, n, u):
        def row_sum(v, hf):
            near = (xa, xb)[hf]
            return (
                full(n, u, (xb, xa, v, hf))
                + U1[n, u, hf, near, v].astype(F32)
                + U2[n, u, hf, v].astype(F32)
            )

        for hf in range(2):
            copies[hf].wait_recv()
            T3[n, u, hf] = row_sum(1 - yh, hf).astype(BF)
        c = push(T3.at[n, u], U3.at[n, u], at_yh)
        for hf in range(2):
            KEEP[n, u, hf] = row_sum(yh, hf)
        return c

    def row_last(copy, n, u, out):
        copy.wait_recv()
        out[:, :, lanes(u)] = (KEEP[n, u] + U3[n, u].astype(F32)).astype(BF)

    def out_grad(lo, hi, k, to):
        def step(j, carry):
            left = H[j].reshape(768, WIDE)
            got = dot(left, CA[k].reshape(768, 512), 0, 0).reshape(2, 8, 16, 512)
            m = MO[k, pl.ds(2 * j, 2)].astype(F32)
            to(j, (got * m[:, None]).reshape(WIDE, 512).astype(BF))
            return carry
        lax.fori_loop(lo, hi, step, 0)

    def far_out(j, v):
        FO[pl.ds(pl.multiple_of(j * WIDE, WIDE), WIDE), :] = v

    def own_out(j, v):
        DO[pl.ds(pl.multiple_of(core * 2048 + j * WIDE, WIDE), WIDE), :] = v

    def in_grad(lo, hi, k, to):
        def step(i, carry):
            d = pl.multiple_of(i * WIDE, WIDE)
            left = TA[k, :, :, :, :, :, pl.ds(d, WIDE)].reshape(768, WIDE)
            for j in range(CHUNKS):
                got = dot(left, G[j].reshape(768, WIDE), 0, 0).reshape(2, 8, 16, WIDE)
                m = MI[k, pl.ds(2 * i, 2), :, WIDE * j : WIDE * (j + 1)].astype(F32)
                to(d, j, (got * m[:, None]).reshape(WIDE, WIDE).astype(BF))
            return carry
        lax.fori_loop(lo, hi, step, 0)

    def far_in(d, j, v):
        FI[pl.ds(d, WIDE), WIDE * j : WIDE * (j + 1)] = v

    def own_in(d, j, v):
        DI[pl.ds(d, WIDE), pl.ds(pl.multiple_of(core * 2048 + WIDE * j, WIDE), WIDE)] = v

    both = range(2)
    for j in range(4):
        d3[0][j].wait_recv()
    for k in both:
        for u in both:
            out_part(H, 0, 4, u, k, wout_of, 0)
    for j in range(4, 8):
        d3[0][j].wait_recv()
    cross0 = []
    for u in both:
        out_part(H, 4, 8, u, other, wout_of, 0)
        cross0.append(row_cross(0, u))
    for j in range(4):
        double_third(1, j, G)
    for u in both:
        out_part(H, 4, 8, u, core, wout_of, 0)
    for j in range(4, 8):
        double_third(1, j, G)
    pair = [row_first(cross0[u], 0, u) for u in both]
    wo_c.wait_send()
    mo_c.wait_recv()
    out_grad(0, 4, other, far_out)
    pair = [row_second(pair[u], 0, u) for u in both]
    out_grad(4, 8, other, far_out)
    dwo_far = push(FO, DO.at[cols(core)], at_core)
    last0 = [row_third(pair[u], 0, u) for u in both]
    for c in cross0:
        c.wait_send()
    for j in range(4):
        d3[1][j].wait_recv()
    for k in both:
        for u in both:
            out_part(G, 0, 4, u, k, win_of, 1)
    for j in range(4, 8):
        d3[1][j].wait_recv()
    cross1 = []
    for u in both:
        out_part(G, 4, 8, u, other, win_of, 1)
        cross1.append(row_cross(1, u))
    for u in both:
        out_part(G, 4, 8, u, core, win_of, 1)
    pair = [row_first(cross1[u], 1, u) for u in both]
    wi_c.wait_send()
    mi_c.wait_recv()
    in_grad(0, 2, other, far_in)
    dwi_far = push(FI, DI.at[:, cols(core)], at_core)
    pair = [row_second(pair[u], 1, u) for u in both]
    in_grad(0, 1, core, own_in)
    last1 = [row_third(pair[u], 1, u) for u in both]
    in_grad(1, 2, core, own_in)
    out_grad(0, 8, core, own_out)
    for u in both:
        row_last(last0[u], 0, u, res_o)
    for u in both:
        row_last(last1[u], 1, u, tg_o)
    dwo_far.wait_recv()
    dwi_far.wait_recv()
    waited = [wo_c, wi_c] + cross0
    for c in sent:
        if not any(c is w for w in waited):
            c.wait_send()


def body(tokens, weight_in, mask_in, weight_out, mask_out, cotangent):
    anywhere = pl.BlockSpec(memory_space=pl.ANY)
    vmem = pl.BlockSpec(memory_space=pltpu.VMEM)
    smem = pl.BlockSpec(memory_space=pltpu.SMEM)

    def halving():
        return [
            pltpu.VMEM((CHUNKS, 2, 2, 96, WIDE), BF),
            pltpu.VMEM((CHUNKS, 2, 2, 96, WIDE), BF),
            pltpu.VMEM((CHUNKS, 2, 2, 96, WIDE), F32),
            pltpu.VMEM((CHUNKS, 2, 96, WIDE), BF),
            pltpu.VMEM((CHUNKS, 2, 96, WIDE), BF),
            pltpu.VMEM((CHUNKS, 96, WIDE), BF),
            pltpu.VMEM((CHUNKS, 96, WIDE), BF),
        ]

    result, tokens_grad, dwi, dwo = pl.pallas_call(
        kernel,
        out_shape=(
            OUT_KIND((2, 48, 512), BF),
            OUT_KIND((2, 48, 512), BF),
            OUT_KIND((512, 4096), BF),
            OUT_KIND((4096, 512), BF),
        ),
        in_specs=[anywhere] * 4 + [smem] * 2,
        out_specs=(vmem,) * 4,
        scratch_shapes=[
            pltpu.VMEM((2, 2, 2, 2, 2, 48, 512), BF),
            pltpu.VMEM((2, 2, 2, 2, 2, 48, 512), BF),
            pltpu.VMEM((2, 512, 2048), BF),
            pltpu.VMEM((2, 2048, 512), BF),
            pltpu.VMEM((512, 2048), BF),
            pltpu.VMEM((2048, 512), BF),
            pltpu.VMEM((4, 16, 2048), BF),
            pltpu.VMEM((2, 4, 16, 2048), BF),
            pltpu.VMEM((16, 16, 512), BF),
            pltpu.VMEM((2, 16, 16, 512), BF),
        ]
        + halving()
        + halving()
        + [
            pltpu.VMEM((CHUNKS, 8, 96, WIDE), BF),
            pltpu.VMEM((CHUNKS, 8, 96, WIDE), BF),
            pltpu.VMEM((2, 2, 2, 2, 2, 2, 48, 256), F32),
            pltpu.VMEM((2, 2, 2, 2, 2, 2, 48, 256), F32),
            pltpu.VMEM((2, 2, 2, 2, 2, 48, 256), BF),
            pltpu.VMEM((2, 2, 2, 2, 2, 48, 256), BF),
            pltpu.VMEM((2, 2, 2, 2, 48, 256), BF),
            pltpu.VMEM((2, 2, 2, 2, 48, 256), BF),
            pltpu.VMEM((2, 2, 2, 48, 256), BF),
            pltpu.VMEM((2, 2, 2, 48, 256), BF),
            pltpu.VMEM((2, 2, 2, 48, 256), F32),
            pltpu.SemaphoreType.DMA((N_COPIES,)),
            pltpu.SemaphoreType.DMA((N_COPIES,)),
            pltpu.SemaphoreType.DMA((8,)),
        ],
        compiler_params=pltpu.CompilerParams(
            collective_id=0, has_side_effects=True, vmem_limit_bytes=VMEM_BYTES
        ),
    )(tokens.reshape(2, 48, 512), cotangent.reshape(2, 48, 512), weight_in, weight_out, mask_in, mask_out.T)
    return result.reshape(96, 512), tokens_grad.reshape(96, 512), dwi, dwo


def solution(mesh):
    return jax.shard_map(
        body,
        mesh=mesh,
        in_specs=(
            P("row", "col"),
            P("col", "row"),
            P("col", "row"),
            P("row", "col"),
            P("row", "col"),
            P("row", "col"),
        ),
        out_specs=(P("row", "col"), P("row", "col"), P("col", "row"), P("row", "col")),
        check_vma=False,
    )
```

time: 154 us -> 138 us (0.90)
  other arithmetic: 8.31 us -> 0 us
  Pallas kernels: 139 us -> 131 us
    pallas_call x1, Pallas kernels: 139 us -> 131 us  [body(): pl.pallas_call(kernel, out_shape=(OUT_KIND((2, 48, 512), BF), OUT_KIND((2...]
    mul x2 -> x0, other arithmetic: 6.94 us -> none  [the longest x1 4.64 us: body(): dwi = (dwi.reshape(4, 8, 16, 4096) * mi[:, None]).reshape(512, 4096)]
    unnamed x17 -> x4, local copies, waits for them, and re-layouts: 2.02 us -> 5.31 us
    broadcast_in_dim x3 -> x0, local copies, waits for them, and re-layouts: 1.77 us -> none  [the longest x1 0.84 us: body(): jnp.broadcast_to(jnp.repeat(mask_out.astype(BF), BLOCK, axis=1)[:, None],...]
where the time goes in v2:
time: 138 us; the launch traced here: 137 us
  Pallas kernels  131 us (95%)
  local copies, waits for them, and re-layouts  5.31 us (4%)
    pallas_call x1, Pallas kernels, body(): pl.pallas_call(kernel, out_shape=(OUT_KIND((2, 48, 512), BF), OUT_KIND((2...  131 us
    unnamed x4, local copies, waits for them, and re-layouts  5.31 us

profile of v2, /device:TPU:0, one launch (start us, length us, event | category | flops | bytes accessed | tf_op | source)
XLA Modules:
  0.0 137.2 jit_solution(5513832749302516354)
XLA Ops:
  0.6 131.2 %shard_map.93 = (bf16[2,48,512]{2,1,0:T(8,128)(2,1)S(1)}, bf16[2,48,512]{2,1,0:T(8,128)(2,1)S(1)}, bf16[512,4096]{1,0:T(8,128)(2,1)S(1)}, bf16[4096,512]{1,0:T(8,128)(2,1)S(1)}) custom-call(bf16[2,48,512]{2,1,0:T(8,128)(2,1)} %bitcast.7, bf16[2,48,512]{2,1,0:T(8,128)(2,1)} %bitcast.8, bf16[512,4096]{1,0:T(8,128)(2,1)} %win.1, bf16[4096,512]{1,0:T(8,128)(2,1)} %wout.1, ...), custom_call_target="tpu_custom_call" | custom-call | tf_op jit(solution)/shard_map/pallas_call | solution.py:521
  131.9 0.6 copy.14
  132.5 0.6 copy.15
  133.2 2.0 %copy.16 = bf16[512,4096]{1,0:T(8,128)(2,1)} copy(bf16[512,4096]{1,0:T(8,128)(2,1)S(1)} %get-tuple-element.14) | data formatting | bytes 8388608
  135.2 2.0 %copy.17 = bf16[4096,512]{1,0:T(8,128)(2,1)} copy(bf16[4096,512]{1,0:T(8,128)(2,1)S(1)} %get-tuple-element.15) | data formatting | bytes 8388608

commit v3 on v2

--- a/solution.py
+++ b/solution.py
@@ -6,15 +6,16 @@
 from jax.sharding import PartitionSpec as P
 
 BLOCK = 128
-CHUNKS = 8
-WIDE = 256
+CHUNKS = 4
+WIDE = 512
 BF = jnp.bfloat16
 F32 = jnp.float32
 
 root_two_pi = 0.7978845608
 cubic_coef = 0.044715
 
-ORDERS = ((0, 2, 1), (1, 2, 0), (2, 0, 1), (0, 1, 2), (1, 0, 2), (2, 1, 0), (0, 2, 1), (1, 2, 0))
+ORDERS = ((0, 1, 2), (1, 2, 0), (2, 0, 1))
+PARTS = 3
 
 
 def dot(left, right, left_dim, right_dim):
@@ -31,10 +32,10 @@
     )
     return value, slope
 OUT_KIND = pltpu.VMEM
-VMEM_BYTES = 49 * 1024 * 1024
-
-
-N_COPIES = 192
+VMEM_BYTES = 53 * 1024 * 1024
+
+
+N_COPIES = 256
 
 
 def kernel(
@@ -127,8 +128,10 @@
     expand_out(core, MO.at[core])
     pl.semaphore_wait(barrier, 7)
 
-    def gather_y(A):
-        return {"y": push(A.at[core, xb, xa, yh], A.at[core, xb, xa, yh], at_yh)}
+    def gather_y(A, c):
+        for hf in range(2):
+            at = A.at[core, xb, xa, yh, hf]
+            c["y%d" % hf] = push(at, at, at_yh)
 
     def gather_first(A, c):
         c["a0"] = push(A.at[core, xb, xa, yh, 0], A.at[core, xb, xa, yh, 0], at_xb)
@@ -141,14 +144,21 @@
         c["B" + tag] = push(A.at[core, xb, :, v, 1], A.at[core, xb, :, v, 1], at_xb)
 
     def gather_third(A, c, v):
-        c["y"].wait_recv()
+        c["y0"].wait_recv()
         c["a1"] = push(A.at[core, xb, xa, v, 0], A.at[core, xb, xa, v, 0], at_xb)
+        c["y1"].wait_recv()
         c["b1"] = push(A.at[core, xb, xa, v, 1], A.at[core, xb, xa, v, 1], at_xa)
 
     def gather_cross(A, c, v, tag):
         c["A" + tag].wait_recv()
+        one = push(A.at[core, :, :, v, 0], A.at[core, :, :, v, 0], at_core)
         c["B" + tag].wait_recv()
-        c["c" + tag] = push(A.at[core, :, :, v], A.at[core, :, :, v], at_core)
+        two = push(A.at[core, :, :, v, 1], A.at[core, :, :, v, 1], at_core)
+        c["c" + tag] = (one, two)
+
+    def crossed(c, tag):
+        for copy in c["c" + tag]:
+            copy.wait_recv()
 
     def mask_in_half(h, m, dst):
         def step(i, carry):
@@ -167,177 +177,164 @@
         lax.fori_loop(0, 16, step, 0)
 
     tok_in.wait()
-    tc = gather_y(TA)
+    tc, cc = {}, {}
+    gather_y(TA, tc)
     gather_first(TA, tc)
-    cot_in.wait()
-    cc = gather_y(CA)
     si_far.wait()
     mask_in_half(other, MIS, FI)
     wi_c = push(FI, WI.at[core], at_core)
     gather_second(TA, tc, yh, "0")
+    cot_in.wait()
     gather_first(CA, cc)
     si_own.wait()
     mask_in_half(core, MI.at[core], WI.at[core])
+    gather_third(TA, tc, 1 - yh)
+    gather_y(CA, cc)
+    gather_cross(TA, tc, yh, "0")
     so_far.wait()
     mask_out_half(other, MOS, FO)
-    gather_cross(TA, tc, yh, "0")
     wo_c = push(FO, WO.at[core], at_core)
-    gather_third(TA, tc, 1 - yh)
     wi_c.wait_recv()
-    tc["c0"].wait_recv()
-
-    def part_rows(j, half, v):
+    crossed(tc, "0")
+
+    def part_in(j, v):
         out = None
         for k in range(2):
-            t = dot(TA[k, half, :, v].reshape(192, 512), WI[k, :, WIDE * j : WIDE * (j + 1)], 1, 0)
+            t = dot(TA[k, :, :, v].reshape(384, 512), WI[k, :, WIDE * j : WIDE * (j + 1)], 1, 0)
             out = t if out is None else out + t
-        return out.reshape(2, 96, WIDE)
-
-    def part_in(j, half):
+        return out.reshape(2, 2, PARTS, 32, WIDE)
+
+    def part_out(j, v):
         out = None
         for k in range(2):
-            t = dot(TA[k, half].reshape(384, 512), WI[k, :, WIDE * j : WIDE * (j + 1)], 1, 0)
+            t = dot(CA[k, :, :, v].reshape(384, 512), WO[k, WIDE * j : WIDE * (j + 1), :], 1, 1)
             out = t if out is None else out + t
-        return out.reshape(2, 2, 96, WIDE)
-
-    def part_out(j, half):
-        out = None
-        for k in range(2):
-            t = dot(CA[k, half].reshape(384, 512), WO[k, WIDE * j : WIDE * (j + 1), :], 1, 1)
-            out = t if out is None else out + t
-        return out.reshape(2, 2, 96, WIDE)
+        return out.reshape(2, 2, PARTS, 32, WIDE)
 
     streams = ((part_in, S1a, R1a, ACa, S2a, R2a, S3a, R3a), (part_out, S1b, R1b, ACb, S2b, R2b, S3b, R3b))
-    first = [[None] * CHUNKS for _ in range(2)]
-    second = [[None] * CHUNKS for _ in range(2)]
-    third = [[None] * CHUNKS for _ in range(2)]
-
-    def halve_rows(j, v):
-        d = ORDERS[j][0]
-        S1a[j, :, v] = part_rows(j, 1 - bits[d], v).astype(BF)
-        c = push(S1a.at[j, :, v], R1a.at[j, :, v], partner[d])
-        first[0][j] = (first[0][j] or ()) + (c,)
-
-    def halve_first(s, j):
+    units = [(j, p) for j in range(CHUNKS) for p in range(PARTS)]
+    first = [{u: () for u in units} for _ in range(2)]
+    second, third = [{}, {}], [{}, {}]
+
+    def halve_first(s, j, v):
         part, S1, R1, AC, S2, R2, S3, R3 = streams[s]
-        d = ORDERS[j][0]
-        S1[j] = part(j, 1 - bits[d]).astype(BF)
-        first[s][j] = (push(S1.at[j], R1.at[j], partner[d]),)
-
-    def halve_kept(s, j):
+        got = part(j, v)
+        for p in range(PARTS):
+            d = ORDERS[p][0]
+            low = bits[d] == 0
+            S1[j, p, :, v] = jnp.where(low, got[1, :, p], got[0, :, p]).astype(BF)
+            c = push(S1.at[j, p, :, v], R1.at[j, p, :, v], partner[d])
+            first[s][j, p] += (c,)
+        for p in range(PARTS):
+            low = bits[ORDERS[p][0]] == 0
+            AC[j, p, :, v] = jnp.where(low, got[0, :, p], got[1, :, p])
+
+    def halve_second(s, j, p):
         part, S1, R1, AC, S2, R2, S3, R3 = streams[s]
-        AC[j] = part(j, bits[ORDERS[j][0]])
-
-    def halve_second(s, j):
+        d = ORDERS[p][1]
+        away, keep = 1 - bits[d], bits[d]
+        for c in first[s][j, p]:
+            c.wait_recv()
+        S2[j, p] = (AC[j, p, away] + R1[j, p, away].astype(F32)).astype(BF)
+        second[s][j, p] = push(S2.at[j, p], R2.at[j, p], partner[d])
+        AC[j, p, keep] = AC[j, p, keep] + R1[j, p, keep].astype(F32)
+
+    def halve_third(s, j, p):
         part, S1, R1, AC, S2, R2, S3, R3 = streams[s]
-        d = ORDERS[j][1]
+        base, d = bits[ORDERS[p][1]], ORDERS[p][2]
         away, keep = 1 - bits[d], bits[d]
-        for c in first[s][j]:
-            c.wait_recv()
-        S2[j] = (AC[j, away] + R1[j, away].astype(F32)).astype(BF)
-        second[s][j] = push(S2.at[j], R2.at[j], partner[d])
-        AC[j, keep] = AC[j, keep] + R1[j, keep].astype(F32)
-
-    def halve_third(s, j):
+        second[s][j, p].wait_recv()
+        S3[j, p] = (AC[j, p, base, away] + R2[j, p, away].astype(F32)).astype(BF)
+        third[s][j, p] = push(S3.at[j, p], R3.at[j, p], partner[d])
+        AC[j, p, base, keep] = AC[j, p, base, keep] + R2[j, p, keep].astype(F32)
+
+    def whole(s, j, p):
         part, S1, R1, AC, S2, R2, S3, R3 = streams[s]
-        base, d = bits[ORDERS[j][1]], ORDERS[j][2]
-        away, keep = 1 - bits[d], bits[d]
-        second[s][j].wait_recv()
-        S3[j] = (AC[j, base, away] + R2[j, away].astype(F32)).astype(BF)
-        third[s][j] = push(S3.at[j], R3.at[j], partner[d])
-        AC[j, base, keep] = AC[j, base, keep] + R2[j, keep].astype(F32)
-
-    def whole(s, j):
-        part, S1, R1, AC, S2, R2, S3, R3 = streams[s]
-        third[s][j].wait_recv()
-        base, last = bits[ORDERS[j][1]], bits[ORDERS[j][2]]
-        return AC[j, base, last] + R3[j].astype(F32), base, last
-
-    d1 = [[None] * CHUNKS for _ in range(2)]
-    d2 = [[None] * CHUNKS for _ in range(2)]
-    d3 = [[None] * CHUNKS for _ in range(2)]
-
-    def double_first(s, j, A):
-        m = [bits[d] for d in ORDERS[j]]
-        at = A.at[j, 4 * m[0] + 2 * m[1] + m[2]]
-        d1[s][j] = push(at, at, partner[ORDERS[j][2]])
-
-    def double_second(s, j, A):
-        m = [bits[d] for d in ORDERS[j]]
-        d1[s][j].wait_recv()
-        at = A.at[j, pl.ds(4 * m[0] + 2 * m[1], 2)]
-        d2[s][j] = push(at, at, partner[ORDERS[j][1]])
-
-    def double_third(s, j, A):
-        m = [bits[d] for d in ORDERS[j]]
-        d2[s][j].wait_recv()
-        at = A.at[j, pl.ds(4 * m[0], 4)]
-        d3[s][j] = push(at, at, partner[ORDERS[j][0]])
-
-    def make_hidden(j):
-        m = [bits[d] for d in ORDERS[j]]
-        v, base, last = whole(0, j)
+        third[s][j, p].wait_recv()
+        base, last = bits[ORDERS[p][1]], bits[ORDERS[p][2]]
+        return AC[j, p, base, last] + R3[j, p].astype(F32), base, last
+
+    d1, d2, d3 = [{}, {}], [{}, {}], [{}, {}]
+
+    def double_first(s, j, p, A):
+        m = [bits[d] for d in ORDERS[p]]
+        at = A.at[j, 4 * m[0] + 2 * m[1] + m[2], p]
+        d1[s][j, p] = push(at, at, partner[ORDERS[p][2]])
+
+    def double_second(s, j, p, A):
+        m = [bits[d] for d in ORDERS[p]]
+        d1[s][j, p].wait_recv()
+        at = A.at[j, pl.ds(4 * m[0] + 2 * m[1], 2), p]
+        d2[s][j, p] = push(at, at, partner[ORDERS[p][1]])
+
+    def double_third(s, j, p, A):
+        m = [bits[d] for d in ORDERS[p]]
+        d2[s][j, p].wait_recv()
+        at = A.at[j, pl.ds(4 * m[0], 4), p]
+        d3[s][j, p] = push(at, at, partner[ORDERS[p][0]])
+
+    def make_hidden(j, p):
+        m = [bits[d] for d in ORDERS[p]]
+        v, base, last = whole(0, j, p)
         value, slope = gelu_both(v)
-        H[j, 4 * m[0] + 2 * m[1] + m[2]] = value.astype(BF)
-        ACa[j, base, last] = slope
-        double_first(0, j, H)
-
-    def make_grad(j):
-        m = [bits[d] for d in ORDERS[j]]
-        v, base, last = whole(1, j)
-        G[j, 4 * m[0] + 2 * m[1] + m[2]] = (v * ACa[j, base, last]).astype(BF)
-        double_first(1, j, G)
-
-    each = range(CHUNKS)
-    for j in range(4):
-        halve_rows(j, yh)
-    gather_second(TA, tc, 1 - yh, "1")
-    for j in range(4, 8):
-        halve_rows(j, yh)
+        H[j, 4 * m[0] + 2 * m[1] + m[2], p] = value.astype(BF)
+        ACa[j, p, base, last] = slope
+        double_first(0, j, p, H)
+
+    def make_grad(j, p):
+        m = [bits[d] for d in ORDERS[p]]
+        v, base, last = whole(1, j, p)
+        G[j, 4 * m[0] + 2 * m[1] + m[2], p] = (v * ACa[j, p, base, last]).astype(BF)
+        double_first(1, j, p, G)
+
+    far = 1 - yh
+    halve_first(0, 0, yh)
+    gather_second(TA, tc, far, "1")
+    halve_first(0, 1, yh)
     gather_second(CA, cc, yh, "0")
-    gather_third(CA, cc, 1 - yh)
-    gather_cross(TA, tc, 1 - yh, "1")
+    halve_first(0, 2, yh)
+    gather_cross(TA, tc, far, "1")
+    halve_first(0, 3, yh)
     so_own.wait()
     mask_out_half(core, MO.at[core], WO.at[core])
-    tc["c1"].wait_recv()
-    for j in range(4):
-        halve_rows(j, 1 - yh)
-    gather_second(CA, cc, 1 - yh, "1")
+    gather_third(CA, cc, far)
     gather_cross(CA, cc, yh, "0")
-    for j in range(4, 8):
-        halve_rows(j, 1 - yh)
-    for j in range(4):
-        halve_kept(0, j)
-    gather_cross(CA, cc, 1 - yh, "1")
+    crossed(tc, "1")
+    halve_first(0, 0, far)
+    halve_first(0, 1, far)
+    gather_second(CA, cc, far, "1")
+    halve_first(0, 2, far)
+    halve_first(0, 3, far)
+    wo_c.wait_recv()
+    crossed(cc, "0")
+    halve_first(1, 0, yh)
+    halve_first(1, 1, yh)
+    gather_cross(CA, cc, far, "1")
     mi_c = push(MIS, MI.at[core], at_core)
     mo_c = push(MOS, MO.at[core], at_core)
-    for j in range(4, 8):
-        halve_kept(0, j)
-    wo_c.wait_recv()
-    cc["c0"].wait_recv()
-    cc["c1"].wait_recv()
-    for j in each:
-        halve_first(1, j)
-    for j in each:
-        halve_second(0, j)
-    for j in each:
-        halve_kept(1, j)
-    for j in each:
-        halve_third(0, j)
-    for j in each:
-        halve_second(1, j)
-    for j in each:
-        make_hidden(j)
-    for j in each:
-        halve_third(1, j)
-    for j in each:
-        double_second(0, j, H)
-    for j in each:
-        make_grad(j)
-    for j in each:
-        double_third(0, j, H)
-    for j in each:
-        double_second(1, j, G)
+    halve_first(1, 2, yh)
+    halve_first(1, 3, yh)
+    crossed(cc, "1")
+    for j in range(CHUNKS):
+        halve_first(1, j, far)
+    for u in units:
+        halve_second(0, *u)
+    for u in units:
+        halve_third(0, *u)
+    for u in units:
+        halve_second(1, *u)
+    for u in units:
+        make_hidden(*u)
+    for u in units:
+        halve_third(1, *u)
+    for u in units:
+        double_second(0, *u, H)
+    for u in units:
+        make_grad(*u)
+    for u in units:
+        double_third(0, *u, H)
+    for u in units:
+        double_second(1, *u, G)
 
     every = slice(None)
 
@@ -398,88 +395,93 @@
         for hf in range(2):
             copies[hf].wait_recv()
             T3[n, u, hf] = row_sum(1 - yh, hf).astype(BF)
-        c = push(T3.at[n, u], U3.at[n, u], at_yh)
-        for hf in range(2):
             KEEP[n, u, hf] = row_sum(yh, hf)
-        return c
+
+    def row_fourth(n, u):
+        return push(T3.at[n, u], U3.at[n, u], at_yh)
 
     def row_last(copy, n, u, out):
         copy.wait_recv()
         out[:, :, lanes(u)] = (KEEP[n, u] + U3[n, u].astype(F32)).astype(BF)
 
-    def out_grad(lo, hi, k, to):
-        def step(j, carry):
-            left = H[j].reshape(768, WIDE)
+    def out_grad(k, to):
+        def step(t, carry):
+            j, c = lax.div(t, 2), pl.multiple_of(256 * lax.rem(t, 2), 256)
+            left = H[j, :, :, :, pl.ds(c, 256)].reshape(768, 256)
             got = dot(left, CA[k].reshape(768, 512), 0, 0).reshape(2, 8, 16, 512)
-            m = MO[k, pl.ds(2 * j, 2)].astype(F32)
-            to(j, (got * m[:, None]).reshape(WIDE, 512).astype(BF))
-            return carry
-        lax.fori_loop(lo, hi, step, 0)
-
-    def far_out(j, v):
-        FO[pl.ds(pl.multiple_of(j * WIDE, WIDE), WIDE), :] = v
-
-    def own_out(j, v):
-        DO[pl.ds(pl.multiple_of(core * 2048 + j * WIDE, WIDE), WIDE), :] = v
+            m = MO[k, pl.ds(2 * t, 2)].astype(F32)
+            to(t, (got * m[:, None]).reshape(256, 512).astype(BF))
+            return carry
+        lax.fori_loop(0, 8, step, 0)
+
+    def far_out(t, v):
+        FO[pl.ds(pl.multiple_of(t * 256, 256), 256), :] = v
+
+    def own_out(t, v):
+        DO[pl.ds(pl.multiple_of(core * 2048 + t * 256, 256), 256), :] = v
 
     def in_grad(lo, hi, k, to):
         def step(i, carry):
-            d = pl.multiple_of(i * WIDE, WIDE)
-            left = TA[k, :, :, :, :, :, pl.ds(d, WIDE)].reshape(768, WIDE)
+            d = pl.multiple_of(i * 256, 256)
+            left = TA[k, :, :, :, :, :, pl.ds(d, 256)].reshape(768, 256)
             for j in range(CHUNKS):
                 got = dot(left, G[j].reshape(768, WIDE), 0, 0).reshape(2, 8, 16, WIDE)
                 m = MI[k, pl.ds(2 * i, 2), :, WIDE * j : WIDE * (j + 1)].astype(F32)
-                to(d, j, (got * m[:, None]).reshape(WIDE, WIDE).astype(BF))
+                to(d, j, (got * m[:, None]).reshape(256, WIDE).astype(BF))
             return carry
         lax.fori_loop(lo, hi, step, 0)
 
     def far_in(d, j, v):
-        FI[pl.ds(d, WIDE), WIDE * j : WIDE * (j + 1)] = v
+        FI[pl.ds(d, 256), WIDE * j : WIDE * (j + 1)] = v
 
     def own_in(d, j, v):
-        DI[pl.ds(d, WIDE), pl.ds(pl.multiple_of(core * 2048 + WIDE * j, WIDE), WIDE)] = v
+        DI[pl.ds(d, 256), pl.ds(pl.multiple_of(core * 2048 + WIDE * j, WIDE), WIDE)] = v
 
     both = range(2)
-    for j in range(4):
-        d3[0][j].wait_recv()
+
+    def arrived(s, lo, hi):
+        for j in range(lo, hi):
+            for p in range(PARTS):
+                d3[s][j, p].wait_recv()
+
+    arrived(0, 0, 2)
     for k in both:
         for u in both:
-            out_part(H, 0, 4, u, k, wout_of, 0)
-    for j in range(4, 8):
-        d3[0][j].wait_recv()
+            out_part(H, 0, 2, u, k, wout_of, 0)
+    arrived(0, 2, 4)
     cross0 = []
     for u in both:
-        out_part(H, 4, 8, u, other, wout_of, 0)
+        out_part(H, 2, 4, u, other, wout_of, 0)
         cross0.append(row_cross(0, u))
-    for j in range(4):
-        double_third(1, j, G)
-    for u in both:
-        out_part(H, 4, 8, u, core, wout_of, 0)
-    for j in range(4, 8):
-        double_third(1, j, G)
+    for u in units[:6]:
+        double_third(1, *u, G)
+    for u in both:
+        out_part(H, 2, 4, u, core, wout_of, 0)
+    for u in units[6:]:
+        double_third(1, *u, G)
     pair = [row_first(cross0[u], 0, u) for u in both]
     wo_c.wait_send()
     mo_c.wait_recv()
-    out_grad(0, 4, other, far_out)
+    out_grad(other, far_out)
+    dwo_far = push(FO, DO.at[cols(core)], at_core)
     pair = [row_second(pair[u], 0, u) for u in both]
-    out_grad(4, 8, other, far_out)
-    dwo_far = push(FO, DO.at[cols(core)], at_core)
-    last0 = [row_third(pair[u], 0, u) for u in both]
+    out_grad(core, own_out)
+    for u in both:
+        row_third(pair[u], 0, u)
     for c in cross0:
         c.wait_send()
-    for j in range(4):
-        d3[1][j].wait_recv()
+    arrived(1, 0, 3)
     for k in both:
         for u in both:
-            out_part(G, 0, 4, u, k, win_of, 1)
-    for j in range(4, 8):
-        d3[1][j].wait_recv()
+            out_part(G, 0, 3, u, k, win_of, 1)
+    arrived(1, 3, 4)
     cross1 = []
     for u in both:
-        out_part(G, 4, 8, u, other, win_of, 1)
+        out_part(G, 3, 4, u, other, win_of, 1)
         cross1.append(row_cross(1, u))
-    for u in both:
-        out_part(G, 4, 8, u, core, win_of, 1)
+    last0 = [row_fourth(0, u) for u in both]
+    for u in both:
+        out_part(G, 3, 4, u, core, win_of, 1)
     pair = [row_first(cross1[u], 1, u) for u in both]
     wi_c.wait_send()
     mi_c.wait_recv()
@@ -487,9 +489,11 @@
     dwi_far = push(FI, DI.at[:, cols(core)], at_core)
     pair = [row_second(pair[u], 1, u) for u in both]
     in_grad(0, 1, core, own_in)
-    last1 = [row_third(pair[u], 1, u) for u in both]
+    last1 = []
+    for u in both:
+        row_third(pair[u], 1, u)
+        last1.append(row_fourth(1, u))
     in_grad(1, 2, core, own_in)
-    out_grad(0, 8, core, own_out)
     for u in both:
         row_last(last0[u], 0, u, res_o)
     for u in both:
@@ -509,13 +513,13 @@
 
     def halving():
         return [
-            pltpu.VMEM((CHUNKS, 2, 2, 96, WIDE), BF),
-            pltpu.VMEM((CHUNKS, 2, 2, 96, WIDE), BF),
-            pltpu.VMEM((CHUNKS, 2, 2, 96, WIDE), F32),
-            pltpu.VMEM((CHUNKS, 2, 96, WIDE), BF),
-            pltpu.VMEM((CHUNKS, 2, 96, WIDE), BF),
-            pltpu.VMEM((CHUNKS, 96, WIDE), BF),
-            pltpu.VMEM((CHUNKS, 96, WIDE), BF),
+            pltpu.VMEM((CHUNKS, PARTS, 2, 2, 32, WIDE), BF),
+            pltpu.VMEM((CHUNKS, PARTS, 2, 2, 32, WIDE), BF),
+            pltpu.VMEM((CHUNKS, PARTS, 2, 2, 32, WIDE), F32),
+            pltpu.VMEM((CHUNKS, PARTS, 2, 32, WIDE), BF),
+            pltpu.VMEM((CHUNKS, PARTS, 2, 32, WIDE), BF),
+            pltpu.VMEM((CHUNKS, PARTS, 32, WIDE), BF),
+            pltpu.VMEM((CHUNKS, PARTS, 32, WIDE), BF),
         ]
 
     result, tokens_grad, dwi, dwo = pl.pallas_call(
@@ -543,8 +547,8 @@
         + halving()
         + halving()
         + [
-            pltpu.VMEM((CHUNKS, 8, 96, WIDE), BF),
-            pltpu.VMEM((CHUNKS, 8, 96, WIDE), BF),
+            pltpu.VMEM((CHUNKS, 8, PARTS, 32, WIDE), BF),
+            pltpu.VMEM((CHUNKS, 8, PARTS, 32, WIDE), BF),
             pltpu.VMEM((2, 2, 2, 2, 2, 2, 48, 256), F32),
             pltpu.VMEM((2, 2, 2, 2, 2, 2, 48, 256), F32),
             pltpu.VMEM((2, 2, 2, 2, 2, 48, 256), BF),

time: 138 us -> 133 us (0.964)
  Pallas kernels: 131 us -> 126 us
    pallas_call x1, Pallas kernels: 131 us -> 126 us  [body(): pl.pallas_call(kernel, out_shape=(OUT_KIND((2, 48, 512), BF), OUT_KIND((2...]
where the time goes in v3:
time: 133 us; the launch traced here: 132 us
  Pallas kernels  126 us (95%)
  local copies, waits for them, and re-layouts  5.31 us (4%)
    pallas_call x1, Pallas kernels, body(): pl.pallas_call(kernel, out_shape=(OUT_KIND((2, 48, 512), BF), OUT_KIND((2...  126 us
    unnamed x4, local copies, waits for them, and re-layouts  5.31 us

profile of v3, /device:TPU:0, one launch (start us, length us, event | category | flops | bytes accessed | tf_op | source)
XLA Modules:
  0.0 132.4 jit_solution(14713780609180176673)
XLA Ops:
  0.6 126.5 %shard_map.93 = (bf16[2,48,512]{2,1,0:T(8,128)(2,1)S(1)}, bf16[2,48,512]{2,1,0:T(8,128)(2,1)S(1)}, bf16[512,4096]{1,0:T(8,128)(2,1)S(1)}, bf16[4096,512]{1,0:T(8,128)(2,1)S(1)}) custom-call(bf16[2,48,512]{2,1,0:T(8,128)(2,1)} %bitcast.7, bf16[2,48,512]{2,1,0:T(8,128)(2,1)} %bitcast.8, bf16[512,4096]{1,0:T(8,128)(2,1)} %win.1, bf16[4096,512]{1,0:T(8,128)(2,1)} %wout.1, ...), custom_call_target="tpu_custom_call" | custom-call | tf_op jit(solution)/shard_map/pallas_call | solution.py:525
  127.1 0.6 copy.14
  127.8 0.6 copy.15
  128.4 2.0 %copy.16 = bf16[512,4096]{1,0:T(8,128)(2,1)} copy(bf16[512,4096]{1,0:T(8,128)(2,1)S(1)} %get-tuple-element.14) | data formatting | bytes 8388608
  130.4 2.0 %copy.17 = bf16[4096,512]{1,0:T(8,128)(2,1)} copy(bf16[4096,512]{1,0:T(8,128)(2,1)S(1)} %get-tuple-element.15) | data formatting | bytes 8388608

commit v4 on v3

--- a/solution.py
+++ b/solution.py
@@ -16,6 +16,10 @@
 
 ORDERS = ((0, 1, 2), (1, 2, 0), (2, 0, 1))
 PARTS = 3
+
+
+def order(j, p):
+    return ORDERS[(j + p) % 3]
 
 
 def dot(left, right, left_dim, right_dim):
@@ -213,6 +217,7 @@
 
     streams = ((part_in, S1a, R1a, ACa, S2a, R2a, S3a, R3a), (part_out, S1b, R1b, ACb, S2b, R2b, S3b, R3b))
     units = [(j, p) for j in range(CHUNKS) for p in range(PARTS)]
+    parted = [(j, p) for p in range(PARTS) for j in range(CHUNKS)]
     first = [{u: () for u in units} for _ in range(2)]
     second, third = [{}, {}], [{}, {}]
 
@@ -220,18 +225,18 @@
         part, S1, R1, AC, S2, R2, S3, R3 = streams[s]
         got = part(j, v)
         for p in range(PARTS):
-            d = ORDERS[p][0]
+            d = order(j, p)[0]
             low = bits[d] == 0
             S1[j, p, :, v] = jnp.where(low, got[1, :, p], got[0, :, p]).astype(BF)
             c = push(S1.at[j, p, :, v], R1.at[j, p, :, v], partner[d])
             first[s][j, p] += (c,)
         for p in range(PARTS):
-            low = bits[ORDERS[p][0]] == 0
+            low = bits[order(j, p)[0]] == 0
             AC[j, p, :, v] = jnp.where(low, got[0, :, p], got[1, :, p])
 
     def halve_second(s, j, p):
         part, S1, R1, AC, S2, R2, S3, R3 = streams[s]
-        d = ORDERS[p][1]
+        d = order(j, p)[1]
         away, keep = 1 - bits[d], bits[d]
         for c in first[s][j, p]:
             c.wait_recv()
@@ -241,7 +246,7 @@
 
     def halve_third(s, j, p):
         part, S1, R1, AC, S2, R2, S3, R3 = streams[s]
-        base, d = bits[ORDERS[p][1]], ORDERS[p][2]
+        base, d = bits[order(j, p)[1]], order(j, p)[2]
         away, keep = 1 - bits[d], bits[d]
         second[s][j, p].wait_recv()
         S3[j, p] = (AC[j, p, base, away] + R2[j, p, away].astype(F32)).astype(BF)
@@ -251,30 +256,30 @@
     def whole(s, j, p):
         part, S1, R1, AC, S2, R2, S3, R3 = streams[s]
         third[s][j, p].wait_recv()
-        base, last = bits[ORDERS[p][1]], bits[ORDERS[p][2]]
+        base, last = bits[order(j, p)[1]], bits[order(j, p)[2]]
         return AC[j, p, base, last] + R3[j, p].astype(F32), base, last
 
     d1, d2, d3 = [{}, {}], [{}, {}], [{}, {}]
 
     def double_first(s, j, p, A):
-        m = [bits[d] for d in ORDERS[p]]
+        m = [bits[d] for d in order(j, p)]
         at = A.at[j, 4 * m[0] + 2 * m[1] + m[2], p]
-        d1[s][j, p] = push(at, at, partner[ORDERS[p][2]])
+        d1[s][j, p] = push(at, at, partner[order(j, p)[2]])
 
     def double_second(s, j, p, A):
-        m = [bits[d] for d in ORDERS[p]]
+        m = [bits[d] for d in order(j, p)]
         d1[s][j, p].wait_recv()
         at = A.at[j, pl.ds(4 * m[0] + 2 * m[1], 2), p]
-        d2[s][j, p] = push(at, at, partner[ORDERS[p][1]])
+        d2[s][j, p] = push(at, at, partner[order(j, p)[1]])
 
     def double_third(s, j, p, A):
-        m = [bits[d] for d in ORDERS[p]]
+        m = [bits[d] for d in order(j, p)]
         d2[s][j, p].wait_recv()
         at = A.at[j, pl.ds(4 * m[0], 4), p]
-        d3[s][j, p] = push(at, at, partner[ORDERS[p][0]])
+        d3[s][j, p] = push(at, at, partner[order(j, p)[0]])
 
     def make_hidden(j, p):
-        m = [bits[d] for d in ORDERS[p]]
+        m = [bits[d] for d in order(j, p)]
         v, base, last = whole(0, j, p)
         value, slope = gelu_both(v)
         H[j, 4 * m[0] + 2 * m[1] + m[2], p] = value.astype(BF)
@@ -282,7 +287,7 @@
         double_first(0, j, p, H)
 
     def make_grad(j, p):
-        m = [bits[d] for d in ORDERS[p]]
+        m = [bits[d] for d in order(j, p)]
         v, base, last = whole(1, j, p)
         G[j, 4 * m[0] + 2 * m[1] + m[2], p] = (v * ACa[j, p, base, last]).astype(BF)
         double_first(1, j, p, G)
@@ -293,27 +298,27 @@
     halve_first(0, 1, yh)
     gather_second(CA, cc, yh, "0")
     halve_first(0, 2, yh)
-    gather_cross(TA, tc, far, "1")
-    halve_first(0, 3, yh)
     so_own.wait()
     mask_out_half(core, MO.at[core], WO.at[core])
+    halve_first(0, 3, yh)
+    gather_cross(CA, cc, yh, "0")
+    gather_cross(TA, tc, far, "1")
+    wo_c.wait_recv()
+    crossed(cc, "0")
+    halve_first(1, 0, yh)
     gather_third(CA, cc, far)
-    gather_cross(CA, cc, yh, "0")
+    halve_first(1, 1, yh)
+    mi_c = push(MIS, MI.at[core], at_core)
+    mo_c = push(MOS, MO.at[core], at_core)
+    halve_first(1, 2, yh)
+    gather_second(CA, cc, far, "1")
+    halve_first(1, 3, yh)
     crossed(tc, "1")
     halve_first(0, 0, far)
     halve_first(0, 1, far)
-    gather_second(CA, cc, far, "1")
+    gather_cross(CA, cc, far, "1")
     halve_first(0, 2, far)
     halve_first(0, 3, far)
-    wo_c.wait_recv()
-    crossed(cc, "0")
-    halve_first(1, 0, yh)
-    halve_first(1, 1, yh)
-    gather_cross(CA, cc, far, "1")
-    mi_c = push(MIS, MI.at[core], at_core)
-    mo_c = push(MOS, MO.at[core], at_core)
-    halve_first(1, 2, yh)
-    halve_first(1, 3, yh)
     crossed(cc, "1")
     for j in range(CHUNKS):
         halve_first(1, j, far)
@@ -323,86 +328,68 @@
         halve_third(0, *u)
     for u in units:
         halve_second(1, *u)
-    for u in units:
+    for u in parted:
         make_hidden(*u)
     for u in units:
         halve_third(1, *u)
-    for u in units:
+    for u in parted:
         double_second(0, *u, H)
-    for u in units:
+    for u in parted:
         make_grad(*u)
-    for u in units:
+    for u in parted:
         double_third(0, *u, H)
-    for u in units:
+    for u in parted:
         double_second(1, *u, G)
 
     every = slice(None)
 
-    def lanes(u):
-        return slice(256 * u, 256 * (u + 1))
-
-    def out_part(A, lo, hi, u, k, weight, right_dim):
-        def step(h, carry):
-            left = jnp.concatenate(
-                [A[i, pl.ds(4 * h, 4)].reshape(384, WIDE) for i in range(lo, hi)], axis=1
-            )
-            got = dot(left, weight(lo, hi, u, k), 1, right_dim).reshape(2, 2, 2, 48, 256)
-            if lo == 0:
-                R[k, u, h] = got
-            else:
-                R[k, u, h] = R[k, u, h] + got
-            return carry
-        lax.fori_loop(0, 2, step, 0)
-
-    def wout_of(lo, hi, u, k):
-        return WO[k, WIDE * lo : WIDE * hi, lanes(u)]
-
-    def win_of(lo, hi, u, k):
-        return WI[k, lanes(u), WIDE * lo : WIDE * hi]
-
-    def row_cross(n, u):
-        return push(R.at[other, u], RX.at[n, u], at_core)
-
-    def full(n, u, idx):
-        return R[(core, u) + idx] + RX[(n, u) + idx]
-
-    def row_first(cross, n, u):
+    def out_part(A, p, k, weight, right_dim):
+        left = jnp.concatenate([A[i, :, p].reshape(256, WIDE) for i in range(CHUNKS)], axis=1)
+        R[k, p] = dot(left, weight[k], 1, right_dim).reshape(2, 2, 2, 2, 16, 512)
+
+    def row_cross(n, p):
+        return push(R.at[other, p], RX.at[n, p], at_core)
+
+    def full(n, p, idx):
+        return R[(core, p) + idx] + RX[(n, p) + idx]
+
+    def row_first(cross, n, p):
         cross.wait_recv()
-        T1[n, u, 0] = full(n, u, (1 - xb, every, every, 0)).astype(BF)
-        a = push(T1.at[n, u, 0], U1.at[n, u, 0], at_xb)
-        T1[n, u, 1] = full(n, u, (every, 1 - xa, every, 1)).astype(BF)
-        b = push(T1.at[n, u, 1], U1.at[n, u, 1], at_xa)
+        T1[n, p, 0] = full(n, p, (1 - xb, every, every, 0)).astype(BF)
+        a = push(T1.at[n, p, 0], U1.at[n, p, 0], at_xb)
+        T1[n, p, 1] = full(n, p, (every, 1 - xa, every, 1)).astype(BF)
+        b = push(T1.at[n, p, 1], U1.at[n, p, 1], at_xa)
         return a, b
 
-    def row_second(copies, n, u):
+    def row_second(copies, n, p):
         copies[0].wait_recv()
-        T2[n, u, 0] = (full(n, u, (xb, 1 - xa, every, 0)) + U1[n, u, 0, 1 - xa].astype(F32)).astype(BF)
-        a = push(T2.at[n, u, 0], U2.at[n, u, 0], at_xa)
+        T2[n, p, 0] = (full(n, p, (xb, 1 - xa, every, 0)) + U1[n, p, 0, 1 - xa].astype(F32)).astype(BF)
+        a = push(T2.at[n, p, 0], U2.at[n, p, 0], at_xa)
         copies[1].wait_recv()
-        T2[n, u, 1] = (full(n, u, (1 - xb, xa, every, 1)) + U1[n, u, 1, 1 - xb].astype(F32)).astype(BF)
-        b = push(T2.at[n, u, 1], U2.at[n, u, 1], at_xb)
+        T2[n, p, 1] = (full(n, p, (1 - xb, xa, every, 1)) + U1[n, p, 1, 1 - xb].astype(F32)).astype(BF)
+        b = push(T2.at[n, p, 1], U2.at[n, p, 1], at_xb)
         return a, b
 
-    def row_third(copies, n, u):
+    def row_third(copies, n, p):
         def row_sum(v, hf):
             near = (xa, xb)[hf]
             return (
-                full(n, u, (xb, xa, v, hf))
-                + U1[n, u, hf, near, v].astype(F32)
-                + U2[n, u, hf, v].astype(F32)
+                full(n, p, (xb, xa, v, hf))
+                + U1[n, p, hf, near, v].astype(F32)
+                + U2[n, p, hf, v].astype(F32)
             )
 
         for hf in range(2):
             copies[hf].wait_recv()
-            T3[n, u, hf] = row_sum(1 - yh, hf).astype(BF)
-            KEEP[n, u, hf] = row_sum(yh, hf)
-
-    def row_fourth(n, u):
-        return push(T3.at[n, u], U3.at[n, u], at_yh)
-
-    def row_last(copy, n, u, out):
+            T3[n, p, hf] = row_sum(1 - yh, hf).astype(BF)
+            KEEP[n, p, hf] = row_sum(yh, hf)
+
+    def row_fourth(n, p):
+        return push(T3.at[n, p], U3.at[n, p], at_yh)
+
+    def row_last(copy, n, p, out):
         copy.wait_recv()
-        out[:, :, lanes(u)] = (KEEP[n, u] + U3[n, u].astype(F32)).astype(BF)
+        out[p] = (KEEP[n, p] + U3[n, p].astype(F32)).astype(BF)
 
     def out_grad(k, to):
         def step(t, carry):
@@ -437,73 +424,91 @@
     def own_in(d, j, v):
         DI[pl.ds(d, 256), pl.ds(pl.multiple_of(core * 2048 + WIDE * j, WIDE), WIDE)] = v
 
-    both = range(2)
-
-    def arrived(s, lo, hi):
-        for j in range(lo, hi):
-            for p in range(PARTS):
-                d3[s][j, p].wait_recv()
-
-    arrived(0, 0, 2)
-    for k in both:
-        for u in both:
-            out_part(H, 0, 2, u, k, wout_of, 0)
-    arrived(0, 2, 4)
-    cross0 = []
-    for u in both:
-        out_part(H, 2, 4, u, other, wout_of, 0)
-        cross0.append(row_cross(0, u))
-    for u in units[:6]:
-        double_third(1, *u, G)
-    for u in both:
-        out_part(H, 2, 4, u, core, wout_of, 0)
-    for u in units[6:]:
-        double_third(1, *u, G)
-    pair = [row_first(cross0[u], 0, u) for u in both]
+    def arrived(s, p):
+        for j in range(CHUNKS):
+            d3[s][j, p].wait_recv()
+
+    cross0, cross1, pair0, pair1 = {}, {}, {}, {}
+
+    def third_of(p):
+        for j in range(CHUNKS):
+            double_third(1, j, p, G)
+
+    for p in range(PARTS):
+        arrived(0, p)
+        out_part(H, p, other, WO, 0)
+        cross0[p] = row_cross(0, p)
+        if p == 2:
+            third_of(0)
+        out_part(H, p, core, WO, 0)
+    third_of(1)
+    pair0[0] = row_first(cross0[0], 0, 0)
+    third_of(2)
+    for p in (1, 2):
+        pair0[p] = row_first(cross0[p], 0, p)
     wo_c.wait_send()
     mo_c.wait_recv()
     out_grad(other, far_out)
     dwo_far = push(FO, DO.at[cols(core)], at_core)
-    pair = [row_second(pair[u], 0, u) for u in both]
+    for p in range(PARTS):
+        pair0[p] = row_second(pair0[p], 0, p)
     out_grad(core, own_out)
-    for u in both:
-        row_third(pair[u], 0, u)
-    for c in cross0:
-        c.wait_send()
-    arrived(1, 0, 3)
-    for k in both:
-        for u in both:
-            out_part(G, 0, 3, u, k, win_of, 1)
-    arrived(1, 3, 4)
-    cross1 = []
-    for u in both:
-        out_part(G, 3, 4, u, other, win_of, 1)
-        cross1.append(row_cross(1, u))
-    last0 = [row_fourth(0, u) for u in both]
-    for u in both:
-        out_part(G, 3, 4, u, core, win_of, 1)
-    pair = [row_first(cross1[u], 1, u) for u in both]
+    for p in range(PARTS):
+        row_third(pair0[p], 0, p)
+        cross0[p].wait_send()
+
+    def row_part(p):
+        arrived(1, p)
+        out_part(G, p, other, WI, 1)
+        cross1[p] = row_cross(1, p)
+
+    row_part(0)
+    out_part(G, 0, core, WI, 1)
+    row_part(1)
+    pair1[0] = row_first(cross1[0], 1, 0)
+    out_part(G, 1, core, WI, 1)
+    row_part(2)
+    last0 = [row_fourth(0, p) for p in range(PARTS)]
+    pair1[1] = row_first(cross1[1], 1, 1)
+    out_part(G, 2, core, WI, 1)
+    pair1[0] = row_second(pair1[0], 1, 0)
+    pair1[2] = row_first(cross1[2], 1, 2)
     wi_c.wait_send()
     mi_c.wait_recv()
-    in_grad(0, 2, other, far_in)
+    in_grad(0, 1, other, far_in)
+    pair1[1] = row_second(pair1[1], 1, 1)
+    row_third(pair1[0], 1, 0)
+    last1 = [row_fourth(1, 0)]
+    in_grad(1, 2, other, far_in)
     dwi_far = push(FI, DI.at[:, cols(core)], at_core)
-    pair = [row_second(pair[u], 1, u) for u in both]
+    pair1[2] = row_second(pair1[2], 1, 2)
+    row_third(pair1[1], 1, 1)
+    last1.append(row_fourth(1, 1))
     in_grad(0, 1, core, own_in)
-    last1 = []
-    for u in both:
-        row_third(pair[u], 1, u)
-        last1.append(row_fourth(1, u))
+    row_third(pair1[2], 1, 2)
+    last1.append(row_fourth(1, 2))
     in_grad(1, 2, core, own_in)
-    for u in both:
-        row_last(last0[u], 0, u, res_o)
-    for u in both:
-        row_last(last1[u], 1, u, tg_o)
+    for p in range(PARTS):
+        row_last(last0[p], 0, p, res_o)
+    for p in range(PARTS):
+        row_last(last1[p], 1, p, tg_o)
     dwo_far.wait_recv()
     dwi_far.wait_recv()
-    waited = [wo_c, wi_c] + cross0
+    waited = [wo_c, wi_c] + list(cross0.values())
     for c in sent:
         if not any(c is w for w in waited):
             c.wait_send()
+
+
+def leave(a, b, c, d, a_o, b_o, c_o, d_o, sem):
+    copies = [
+        pltpu.make_async_copy(src, dst, sem.at[k])
+        for k, (src, dst) in enumerate(((c, c_o), (d, d_o), (a, a_o), (b, b_o)))
+    ]
+    for copy in copies:
+        copy.start()
+    for copy in copies:
+        copy.wait()
 
 
 def body(tokens, weight_in, mask_in, weight_out, mask_out, cotangent):
@@ -522,11 +527,11 @@
             pltpu.VMEM((CHUNKS, PARTS, 32, WIDE), BF),
         ]
 
-    result, tokens_grad, dwi, dwo = pl.pallas_call(
+    held = pl.pallas_call(
         kernel,
         out_shape=(
-            OUT_KIND((2, 48, 512), BF),
-            OUT_KIND((2, 48, 512), BF),
+            OUT_KIND((PARTS, 2, 16, 512), BF),
+            OUT_KIND((PARTS, 2, 16, 512), BF),
             OUT_KIND((512, 4096), BF),
             OUT_KIND((4096, 512), BF),
         ),
@@ -549,15 +554,15 @@
         + [
             pltpu.VMEM((CHUNKS, 8, PARTS, 32, WIDE), BF),
             pltpu.VMEM((CHUNKS, 8, PARTS, 32, WIDE), BF),
-            pltpu.VMEM((2, 2, 2, 2, 2, 2, 48, 256), F32),
-            pltpu.VMEM((2, 2, 2, 2, 2, 2, 48, 256), F32),
-            pltpu.VMEM((2, 2, 2, 2, 2, 48, 256), BF),
-            pltpu.VMEM((2, 2, 2, 2, 2, 48, 256), BF),
-            pltpu.VMEM((2, 2, 2, 2, 48, 256), BF),
-            pltpu.VMEM((2, 2, 2, 2, 48, 256), BF),
-            pltpu.VMEM((2, 2, 2, 48, 256), BF),
-            pltpu.VMEM((2, 2, 2, 48, 256), BF),
-            pltpu.VMEM((2, 2, 2, 48, 256), F32),
+            pltpu.VMEM((2, PARTS, 2, 2, 2, 2, 16, 512), F32),
+            pltpu.VMEM((2, PARTS, 2, 2, 2, 2, 16, 512), F32),
+            pltpu.VMEM((2, PARTS, 2, 2, 2, 16, 512), BF),
+            pltpu.VMEM((2, PARTS, 2, 2, 2, 16, 512), BF),
+            pltpu.VMEM((2, PARTS, 2, 2, 16, 512), BF),
+            pltpu.VMEM((2, PARTS, 2, 2, 16, 512), BF),
+            pltpu.VMEM((2, PARTS, 2, 16, 512), BF),
+            pltpu.VMEM((2, PARTS, 2, 16, 512), BF),
+            pltpu.VMEM((2, PARTS, 2, 16, 512), F32),
             pltpu.SemaphoreType.DMA((N_COPIES,)),
             pltpu.SemaphoreType.DMA((N_COPIES,)),
             pltpu.SemaphoreType.DMA((8,)),
@@ -566,6 +571,15 @@
             collective_id=0, has_side_effects=True, vmem_limit_bytes=VMEM_BYTES
         ),
     )(tokens.reshape(2, 48, 512), cotangent.reshape(2, 48, 512), weight_in, weight_out, mask_in, mask_out.T)
+    shapes = ((PARTS, 2, 16, 512), (PARTS, 2, 16, 512), (512, 4096), (4096, 512))
+    result, tokens_grad, dwi, dwo = pl.pallas_call(
+        leave,
+        out_shape=tuple(jax.ShapeDtypeStruct(shape, BF) for shape in shapes),
+        in_specs=[anywhere] * 4,
+        out_specs=(anywhere,) * 4,
+        scratch_shapes=[pltpu.SemaphoreType.DMA((4,))],
+        compiler_params=pltpu.CompilerParams(vmem_limit_bytes=1024 * 1024),
+    )(*held)
     return result.reshape(96, 512), tokens_grad.reshape(96, 512), dwi, dwo
 
 

time: 133 us -> 128 us (0.962)
  local copies, waits for them, and re-layouts: 5.31 us -> 0 us
    unnamed x4 -> x0, local copies, waits for them, and re-layouts: 5.31 us -> none
    pallas_call x1 -> x2, Pallas kernels: 126 us -> 127 us  [the longest x1 124 us: body(): pl.pallas_call(kernel, out_shape=(OUT_KIND((PARTS, 2, 16, 512), BF), OUT_...]
where the time goes in v4:
time: 128 us
  Pallas kernels  127 us (99%)
    pallas_call x1, Pallas kernels, body(): pl.pallas_call(kernel, out_shape=(OUT_KIND((PARTS, 2, 16, 512), BF), OUT_...  124 us
    pallas_call x1, Pallas kernels, body(): pl.pallas_call(leave, out_shape=tuple((jax.ShapeDtypeStruct(shape, BF) fo...  3.43 us

profile of v4, /device:TPU:0, one launch (start us, length us, event | category | flops | bytes accessed | tf_op | source)
XLA Modules:
  0.0 128.1 jit_solution(17325097960831412593)
XLA Ops:
  0.6 123.9 %shard_map.93 = (bf16[3,2,16,512]{3,2,1,0:T(8,128)(2,1)S(1)}, bf16[3,2,16,512]{3,2,1,0:T(8,128)(2,1)S(1)}, bf16[512,4096]{1,0:T(8,128)(2,1)S(1)}, bf16[4096,512]{1,0:T(8,128)(2,1)S(1)}) custom-call(bf16[2,48,512]{2,1,0:T(8,128)(2,1)} %bitcast.5, bf16[2,48,512]{2,1,0:T(8,128)(2,1)} %bitcast.6, bf16[512,4096]{1,0:T(8,128)(2,1)} %win.1, ...), custom_call_target="tpu_custom_call" | custom-call | tf_op jit(solution)/shard_map/pallas_call | solution.py:530
  124.5 3.4 %shard_map.94 = (bf16[3,2,16,512]{3,2,1,0:T(8,128)(2,1)}, bf16[3,2,16,512]{3,2,1,0:T(8,128)(2,1)}, bf16[512,4096]{1,0:T(8,128)(2,1)}, bf16[4096,512]{1,0:T(8,128)(2,1)}) custom-call(bf16[3,2,16,512]{3,2,1,0:T(8,128)(2,1)S(1)} %get-tuple-element.12.a, bf16[3,2,16,512]{3,2,1,0:T(8,128)(2,1)S(1)} %get-tuple-element.13.b, ...), custom_call_target="tpu_custom_call" | custom-call | tf_op jit(solution)/shard_map/pallas_call | solution.py:575

commit v5 on v4

--- a/solution.py
+++ b/solution.py
@@ -180,21 +180,22 @@
             return carry
         lax.fori_loop(0, 16, step, 0)
 
+    far = 1 - yh
     tok_in.wait()
     tc, cc = {}, {}
     gather_y(TA, tc)
     gather_first(TA, tc)
+    cot_in.wait()
+    gather_y(CA, cc)
     si_far.wait()
     mask_in_half(other, MIS, FI)
     wi_c = push(FI, WI.at[core], at_core)
     gather_second(TA, tc, yh, "0")
-    cot_in.wait()
     gather_first(CA, cc)
     si_own.wait()
     mask_in_half(core, MI.at[core], WI.at[core])
-    gather_third(TA, tc, 1 - yh)
-    gather_y(CA, cc)
     gather_cross(TA, tc, yh, "0")
+    gather_second(CA, cc, yh, "0")
     so_far.wait()
     mask_out_half(other, MOS, FO)
     wo_c = push(FO, WO.at[core], at_core)
@@ -292,33 +293,31 @@
         G[j, 4 * m[0] + 2 * m[1] + m[2], p] = (v * ACa[j, p, base, last]).astype(BF)
         double_first(1, j, p, G)
 
-    far = 1 - yh
     halve_first(0, 0, yh)
+    gather_third(TA, tc, far)
+    halve_first(0, 1, yh)
+    gather_third(CA, cc, far)
+    halve_first(0, 2, yh)
+    gather_cross(CA, cc, yh, "0")
+    halve_first(0, 3, yh)
     gather_second(TA, tc, far, "1")
-    halve_first(0, 1, yh)
-    gather_second(CA, cc, yh, "0")
-    halve_first(0, 2, yh)
     so_own.wait()
     mask_out_half(core, MO.at[core], WO.at[core])
-    halve_first(0, 3, yh)
-    gather_cross(CA, cc, yh, "0")
-    gather_cross(TA, tc, far, "1")
     wo_c.wait_recv()
     crossed(cc, "0")
     halve_first(1, 0, yh)
-    gather_third(CA, cc, far)
+    gather_second(CA, cc, far, "1")
     halve_first(1, 1, yh)
+    gather_cross(TA, tc, far, "1")
+    halve_first(1, 2, yh)
+    halve_first(1, 3, yh)
     mi_c = push(MIS, MI.at[core], at_core)
     mo_c = push(MOS, MO.at[core], at_core)
-    halve_first(1, 2, yh)
-    gather_second(CA, cc, far, "1")
-    halve_first(1, 3, yh)
     crossed(tc, "1")
     halve_first(0, 0, far)
-    halve_first(0, 1, far)
     gather_cross(CA, cc, far, "1")
-    halve_first(0, 2, far)
-    halve_first(0, 3, far)
+    for j in range(1, CHUNKS):
+        halve_first(0, j, far)
     crossed(cc, "1")
     for j in range(CHUNKS):
         halve_first(1, j, far)
@@ -479,15 +478,14 @@
     pair1[1] = row_second(pair1[1], 1, 1)
     row_third(pair1[0], 1, 0)
     last1 = [row_fourth(1, 0)]
+    pair1[2] = row_second(pair1[2], 1, 2)
     in_grad(1, 2, other, far_in)
     dwi_far = push(FI, DI.at[:, cols(core)], at_core)
-    pair1[2] = row_second(pair1[2], 1, 2)
     row_third(pair1[1], 1, 1)
     last1.append(row_fourth(1, 1))
-    in_grad(0, 1, core, own_in)
     row_third(pair1[2], 1, 2)
     last1.append(row_fourth(1, 2))
-    in_grad(1, 2, core, own_in)
+    in_grad(0, 2, core, own_in)
     for p in range(PARTS):
         row_last(last0[p], 0, p, res_o)
     for p in range(PARTS):
@@ -501,10 +499,12 @@
 
 
 def leave(a, b, c, d, a_o, b_o, c_o, d_o, sem):
-    copies = [
-        pltpu.make_async_copy(src, dst, sem.at[k])
-        for k, (src, dst) in enumerate(((c, c_o), (d, d_o), (a, a_o), (b, b_o)))
-    ]
+    pairs = []
+    for i in range(4):
+        pairs.append((c.at[pl.ds(128 * i, 128)], c_o.at[pl.ds(128 * i, 128)]))
+        pairs.append((d.at[pl.ds(1024 * i, 1024)], d_o.at[pl.ds(1024 * i, 1024)]))
+    pairs += [(a, a_o), (b, b_o)]
+    copies = [pltpu.make_async_copy(src, dst, sem.at[k]) for k, (src, dst) in enumerate(pairs)]
     for copy in copies:
         copy.start()
     for copy in copies:
@@ -577,7 +577,7 @@
         out_shape=tuple(jax.ShapeDtypeStruct(shape, BF) for shape in shapes),
         in_specs=[anywhere] * 4,
         out_specs=(anywhere,) * 4,
-        scratch_shapes=[pltpu.SemaphoreType.DMA((4,))],
+        scratch_shapes=[pltpu.SemaphoreType.DMA((10,))],
         compiler_params=pltpu.CompilerParams(vmem_limit_bytes=1024 * 1024),
     )(*held)
     return result.reshape(96, 512), tokens_grad.reshape(96, 512), dwi, dwo

time: 128 us -> 126 us (0.984)
  Pallas kernels: 127 us -> 125 us
    pallas_call x1, Pallas kernels: 124 us -> 122 us  [body(): pl.pallas_call(kernel, out_shape=(OUT_KIND((PARTS, 2, 16, 512), BF), OUT_...]
where the time goes in v5:
time: 126 us
  Pallas kernels  125 us (99%)
    pallas_call x1, Pallas kernels, body(): pl.pallas_call(kernel, out_shape=(OUT_KIND((PARTS, 2, 16, 512), BF), OUT_...  122 us
    pallas_call x1, Pallas kernels, body(): pl.pallas_call(leave, out_shape=tuple((jax.ShapeDtypeStruct(shape, BF) fo...  3.4 us

profile of v5, /device:TPU:0, one launch (start us, length us, event | category | flops | bytes accessed | tf_op | source)
XLA Modules:
  0.0 126.3 jit_solution(2898151791919225987)
XLA Ops:
  0.6 122.0 %shard_map.93 = (bf16[3,2,16,512]{3,2,1,0:T(8,128)(2,1)S(1)}, bf16[3,2,16,512]{3,2,1,0:T(8,128)(2,1)S(1)}, bf16[512,4096]{1,0:T(8,128)(2,1)S(1)}, bf16[4096,512]{1,0:T(8,128)(2,1)S(1)}) custom-call(bf16[2,48,512]{2,1,0:T(8,128)(2,1)} %bitcast.5, bf16[2,48,512]{2,1,0:T(8,128)(2,1)} %bitcast.6, bf16[512,4096]{1,0:T(8,128)(2,1)} %win.1, ...), custom_call_target="tpu_custom_call" | custom-call | tf_op jit(solution)/shard_map/pallas_call | solution.py:530
  122.7 3.4 %shard_map.94 = (bf16[3,2,16,512]{3,2,1,0:T(8,128)(2,1)}, bf16[3,2,16,512]{3,2,1,0:T(8,128)(2,1)}, bf16[512,4096]{1,0:T(8,128)(2,1)}, bf16[4096,512]{1,0:T(8,128)(2,1)}) custom-call(bf16[3,2,16,512]{3,2,1,0:T(8,128)(2,1)S(1)} %get-tuple-element.12.a, bf16[3,2,16,512]{3,2,1,0:T(8,128)(2,1)S(1)} %get-tuple-element.13.b, ...), custom_call_target="tpu_custom_call" | custom-call | tf_op jit(solution)/shard_map/pallas_call | solution.py:575

commit v6 on v5

--- a/solution.py
+++ b/solution.py
@@ -39,7 +39,7 @@
 VMEM_BYTES = 53 * 1024 * 1024
 
 
-N_COPIES = 256
+N_COPIES = 288
 
 
 def kernel(
@@ -48,7 +48,7 @@
     TA, CA, WI, WO, FI, FO, MIS, MI, MOS, MO,
     S1a, R1a, ACa, S2a, R2a, S3a, R3a,
     S1b, R1b, ACb, S2b, R2b, S3b, R3b,
-    H, G, R, RX, T1, U1, T2, U2, T3, U3, KEEP,
+    H, G, R, RX, T1, U1, T2, U2, KEEP,
     send_sem, recv_sem, local_sem,
 ):
     row = lax.axis_index("row")
@@ -67,6 +67,8 @@
     at_xa = {"row": row + 2 * (1 - 2 * lax.rem(x, 2)), "col": col}
     at_xb = {"row": row + 2 * (3 - 2 * x), "col": col}
     at_yh = {"row": row + 1 - 2 * yh, "col": col}
+    at_xa_yh = {"row": at_xa["row"] + 1 - 2 * yh, "col": col}
+    at_xb_yh = {"row": at_xb["row"] + 1 - 2 * yh, "col": col}
     bits = (yl, za, zb)
     partner = (at_y, at_za, at_zb)
 
@@ -97,7 +99,7 @@
         return pl.ds(pl.multiple_of(h * 2048, 2048), 2048)
 
     barrier = pltpu.get_barrier_semaphore()
-    for where in (at_core, at_y, at_za, at_zb, at_xa, at_xb, at_yh):
+    for where in (at_core, at_y, at_za, at_zb, at_xa, at_xb, at_yh, at_xa_yh, at_xb_yh):
         pl.semaphore_signal(barrier, inc=1, device_id=where, device_id_type=pl.DeviceIdType.MESH)
 
     tok_in = local(tok, TA.at[core, xb, xa, yh])
@@ -130,7 +132,7 @@
     expand_in(core, MI.at[core])
     expand_out(other, MOS)
     expand_out(core, MO.at[core])
-    pl.semaphore_wait(barrier, 7)
+    pl.semaphore_wait(barrier, 9)
 
     def gather_y(A, c):
         for hf in range(2):
@@ -362,33 +364,27 @@
 
     def row_second(copies, n, p):
         copies[0].wait_recv()
-        T2[n, p, 0] = (full(n, p, (xb, 1 - xa, every, 0)) + U1[n, p, 0, 1 - xa].astype(F32)).astype(BF)
-        a = push(T2.at[n, p, 0], U2.at[n, p, 0], at_xa)
+        T2[n, p, 0] = (full(n, p, (xb, every, every, 0)) + U1[n, p, 0].astype(F32)).astype(BF)
+        KEEP[n, p, 0] = full(n, p, (xb, xa, yh, 0)) + U1[n, p, 0, xa, yh].astype(F32)
         copies[1].wait_recv()
-        T2[n, p, 1] = (full(n, p, (1 - xb, xa, every, 1)) + U1[n, p, 1, 1 - xb].astype(F32)).astype(BF)
-        b = push(T2.at[n, p, 1], U2.at[n, p, 1], at_xb)
-        return a, b
-
-    def row_third(copies, n, p):
-        def row_sum(v, hf):
-            near = (xa, xb)[hf]
-            return (
-                full(n, p, (xb, xa, v, hf))
-                + U1[n, p, hf, near, v].astype(F32)
-                + U2[n, p, hf, v].astype(F32)
-            )
-
-        for hf in range(2):
-            copies[hf].wait_recv()
-            T3[n, p, hf] = row_sum(1 - yh, hf).astype(BF)
-            KEEP[n, p, hf] = row_sum(yh, hf)
-
-    def row_fourth(n, p):
-        return push(T3.at[n, p], U3.at[n, p], at_yh)
-
-    def row_last(copy, n, p, out):
-        copy.wait_recv()
-        out[p] = (KEEP[n, p] + U3[n, p].astype(F32)).astype(BF)
+        T2[n, p, 1] = (full(n, p, (every, xa, every, 1)) + U1[n, p, 1].astype(F32)).astype(BF)
+        KEEP[n, p, 1] = full(n, p, (xb, xa, yh, 1)) + U1[n, p, 1, xb, yh].astype(F32)
+
+    def row_direct(n, p):
+        got = []
+        for hf, mine, side, corner in ((0, xa, at_xa, at_xa_yh), (1, xb, at_xb, at_xb_yh)):
+            got.append(push(T2.at[n, p, hf, 1 - mine, 1 - yh], U2.at[n, p, hf, 0], corner))
+            got.append(push(T2.at[n, p, hf, mine, 1 - yh], U2.at[n, p, hf, 1], at_yh))
+            got.append(push(T2.at[n, p, hf, 1 - mine, yh], U2.at[n, p, hf, 2], side))
+        return got
+
+    def row_last(copies, n, p, out):
+        for copy in copies:
+            copy.wait_recv()
+        total = KEEP[n, p]
+        for k in range(3):
+            total = total + U2[n, p, :, k].astype(F32)
+        out[p] = total.astype(BF)
 
     def out_grad(k, to):
         def step(t, carry):
@@ -450,11 +446,9 @@
     out_grad(other, far_out)
     dwo_far = push(FO, DO.at[cols(core)], at_core)
     for p in range(PARTS):
-        pair0[p] = row_second(pair0[p], 0, p)
+        row_second(pair0[p], 0, p)
+        cross0[p].wait_send()
     out_grad(core, own_out)
-    for p in range(PARTS):
-        row_third(pair0[p], 0, p)
-        cross0[p].wait_send()
 
     def row_part(p):
         arrived(1, p)
@@ -467,24 +461,22 @@
     pair1[0] = row_first(cross1[0], 1, 0)
     out_part(G, 1, core, WI, 1)
     row_part(2)
-    last0 = [row_fourth(0, p) for p in range(PARTS)]
+    last0 = [row_direct(0, p) for p in range(PARTS)]
     pair1[1] = row_first(cross1[1], 1, 1)
     out_part(G, 2, core, WI, 1)
-    pair1[0] = row_second(pair1[0], 1, 0)
+    last1 = []
+    row_second(pair1[0], 1, 0)
+    last1.append(row_direct(1, 0))
     pair1[2] = row_first(cross1[2], 1, 2)
     wi_c.wait_send()
     mi_c.wait_recv()
     in_grad(0, 1, other, far_in)
-    pair1[1] = row_second(pair1[1], 1, 1)
-    row_third(pair1[0], 1, 0)
-    last1 = [row_fourth(1, 0)]
-    pair1[2] = row_second(pair1[2], 1, 2)
+    row_second(pair1[1], 1, 1)
+    last1.append(row_direct(1, 1))
     in_grad(1, 2, other, far_in)
     dwi_far = push(FI, DI.at[:, cols(core)], at_core)
-    row_third(pair1[1], 1, 1)
-    last1.append(row_fourth(1, 1))
-    row_third(pair1[2], 1, 2)
-    last1.append(row_fourth(1, 2))
+    row_second(pair1[2], 1, 2)
+    last1.append(row_direct(1, 2))
     in_grad(0, 2, core, own_in)
     for p in range(PARTS):
         row_last(last0[p], 0, p, res_o)
@@ -558,10 +550,8 @@
             pltpu.VMEM((2, PARTS, 2, 2, 2, 2, 16, 512), F32),
             pltpu.VMEM((2, PARTS, 2, 2, 2, 16, 512), BF),
             pltpu.VMEM((2, PARTS, 2, 2, 2, 16, 512), BF),
-            pltpu.VMEM((2, PARTS, 2, 2, 16, 512), BF),
-            pltpu.VMEM((2, PARTS, 2, 2, 16, 512), BF),
-            pltpu.VMEM((2, PARTS, 2, 16, 512), BF),
-            pltpu.VMEM((2, PARTS, 2, 16, 512), BF),
+            pltpu.VMEM((2, PARTS, 2, 2, 2, 16, 512), BF),
+            pltpu.VMEM((2, PARTS, 2, 3, 16, 512), BF),
             pltpu.VMEM((2, PARTS, 2, 16, 512), F32),
             pltpu.SemaphoreType.DMA((N_COPIES,)),
             pltpu.SemaphoreType.DMA((N_COPIES,)),

time: 126 us -> 125 us (level)
    pallas_call x1, Pallas kernels: 122 us -> 120 us  [body(): pl.pallas_call(kernel, out_shape=(OUT_KIND((PARTS, 2, 16, 512), BF), OUT_...]
where the time goes in v6:
time: 125 us
  Pallas kernels  124 us (99%)
    pallas_call x1, Pallas kernels, body(): pl.pallas_call(kernel, out_shape=(OUT_KIND((PARTS, 2, 16, 512), BF), OUT_...  120 us
    pallas_call x1, Pallas kernels, body(): pl.pallas_call(leave, out_shape=tuple((jax.ShapeDtypeStruct(shape, BF) fo...  3.4 us

profile of v6, /device:TPU:0, one launch (start us, length us, event | category | flops | bytes accessed | tf_op | source)
XLA Modules:
  0.0 124.5 jit_solution(2391924224626278500)
XLA Ops:
  0.6 120.3 %shard_map.93 = (bf16[3,2,16,512]{3,2,1,0:T(8,128)(2,1)S(1)}, bf16[3,2,16,512]{3,2,1,0:T(8,128)(2,1)S(1)}, bf16[512,4096]{1,0:T(8,128)(2,1)S(1)}, bf16[4096,512]{1,0:T(8,128)(2,1)S(1)}) custom-call(bf16[2,48,512]{2,1,0:T(8,128)(2,1)} %bitcast.5, bf16[2,48,512]{2,1,0:T(8,128)(2,1)} %bitcast.6, bf16[512,4096]{1,0:T(8,128)(2,1)} %win.1, ...), custom_call_target="tpu_custom_call" | custom-call | tf_op jit(solution)/shard_map/pallas_call | solution.py:522
  121.0 3.4 %shard_map.94 = (bf16[3,2,16,512]{3,2,1,0:T(8,128)(2,1)}, bf16[3,2,16,512]{3,2,1,0:T(8,128)(2,1)}, bf16[512,4096]{1,0:T(8,128)(2,1)}, bf16[4096,512]{1,0:T(8,128)(2,1)}) custom-call(bf16[3,2,16,512]{3,2,1,0:T(8,128)(2,1)S(1)} %get-tuple-element.12.a, bf16[3,2,16,512]{3,2,1,0:T(8,128)(2,1)S(1)} %get-tuple-element.13.b, ...), custom_call_target="tpu_custom_call" | custom-call | tf_op jit(solution)/shard_map/pallas_call | solution.py:565

commit v7 on v6

--- a/solution.py
+++ b/solution.py
@@ -378,6 +378,36 @@
             got.append(push(T2.at[n, p, hf, 1 - mine, yh], U2.at[n, p, hf, 2], side))
         return got
 
+    def result_second(copies, p):
+        copies[0].wait_recv()
+        T2[0, p, 0, 0] = (full(0, p, (xb, 1 - xa, every, 0)) + U1[0, p, 0, 1 - xa].astype(F32)).astype(BF)
+        a = push(T2.at[0, p, 0, 0], U2.at[0, p, 0, pl.ds(0, 2)], at_xa)
+        copies[1].wait_recv()
+        T2[0, p, 1, 0] = (full(0, p, (1 - xb, xa, every, 1)) + U1[0, p, 1, 1 - xb].astype(F32)).astype(BF)
+        b = push(T2.at[0, p, 1, 0], U2.at[0, p, 1, pl.ds(0, 2)], at_xb)
+        return a, b
+
+    def result_third(copies, p):
+        def row_sum(v, hf):
+            near = (xa, xb)[hf]
+            return (
+                full(0, p, (xb, xa, v, hf))
+                + U1[0, p, hf, near, v].astype(F32)
+                + U2[0, p, hf, v].astype(F32)
+            )
+
+        for hf in range(2):
+            copies[hf].wait_recv()
+            T2[0, p, hf, 1, 0] = row_sum(1 - yh, hf).astype(BF)
+            KEEP[0, p, hf] = row_sum(yh, hf)
+
+    def result_fourth(p):
+        return push(T2.at[0, p, :, 1, 0], U2.at[0, p, :, 2], at_yh)
+
+    def result_last(copy, p):
+        copy.wait_recv()
+        res_o[p] = (KEEP[0, p] + U2[0, p, :, 2].astype(F32)).astype(BF)
+
     def row_last(copies, n, p, out):
         for copy in copies:
             copy.wait_recv()
@@ -446,9 +476,11 @@
     out_grad(other, far_out)
     dwo_far = push(FO, DO.at[cols(core)], at_core)
     for p in range(PARTS):
-        row_second(pair0[p], 0, p)
+        pair0[p] = result_second(pair0[p], p)
+    out_grad(core, own_out)
+    for p in range(PARTS):
+        result_third(pair0[p], p)
         cross0[p].wait_send()
-    out_grad(core, own_out)
 
     def row_part(p):
         arrived(1, p)
@@ -461,7 +493,7 @@
     pair1[0] = row_first(cross1[0], 1, 0)
     out_part(G, 1, core, WI, 1)
     row_part(2)
-    last0 = [row_direct(0, p) for p in range(PARTS)]
+    last0 = [result_fourth(p) for p in range(PARTS)]
     pair1[1] = row_first(cross1[1], 1, 1)
     out_part(G, 2, core, WI, 1)
     last1 = []
@@ -479,7 +511,7 @@
     last1.append(row_direct(1, 2))
     in_grad(0, 2, core, own_in)
     for p in range(PARTS):
-        row_last(last0[p], 0, p, res_o)
+        result_last(last0[p], p)
     for p in range(PARTS):
         row_last(last1[p], 1, p, tg_o)
     dwo_far.wait_recv()

time: 125 us -> 125 us (level)
  no operation moved by 1% of the time
where the time goes in v7:
time: 125 us
  Pallas kernels  124 us (99%)
    pallas_call x1, Pallas kernels, body(): pl.pallas_call(kernel, out_shape=(OUT_KIND((PARTS, 2, 16, 512), BF), OUT_...  121 us
    pallas_call x1, Pallas kernels, body(): pl.pallas_call(leave, out_shape=tuple((jax.ShapeDtypeStruct(shape, BF) fo...  3.4 us

profile of v7, /device:TPU:0, one launch (start us, length us, event | category | flops | bytes accessed | tf_op | source)
XLA Modules:
  0.0 124.8 jit_solution(10661857574498055536)
XLA Ops:
  0.6 120.6 %shard_map.93 = (bf16[3,2,16,512]{3,2,1,0:T(8,128)(2,1)S(1)}, bf16[3,2,16,512]{3,2,1,0:T(8,128)(2,1)S(1)}, bf16[512,4096]{1,0:T(8,128)(2,1)S(1)}, bf16[4096,512]{1,0:T(8,128)(2,1)S(1)}) custom-call(bf16[2,48,512]{2,1,0:T(8,128)(2,1)} %bitcast.5, bf16[2,48,512]{2,1,0:T(8,128)(2,1)} %bitcast.6, bf16[512,4096]{1,0:T(8,128)(2,1)} %win.1, ...), custom_call_target="tpu_custom_call" | custom-call | tf_op jit(solution)/shard_map/pallas_call | solution.py:554
  121.3 3.4 %shard_map.94 = (bf16[3,2,16,512]{3,2,1,0:T(8,128)(2,1)}, bf16[3,2,16,512]{3,2,1,0:T(8,128)(2,1)}, bf16[512,4096]{1,0:T(8,128)(2,1)}, bf16[4096,512]{1,0:T(8,128)(2,1)}) custom-call(bf16[3,2,16,512]{3,2,1,0:T(8,128)(2,1)S(1)} %get-tuple-element.12.a, bf16[3,2,16,512]{3,2,1,0:T(8,128)(2,1)S(1)} %get-tuple-element.13.b, ...), custom_call_target="tpu_custom_call" | custom-call | tf_op jit(solution)/shard_map/pallas_call | solution.py:597
